TPU v7x, 32 devices: a whole 2x2x4 slice. The times are simulated.
32 devices in a mesh: index: 8 (over y, x, core), query: 4 (over z).
Axes of the slice: x: 2, y: 2, z: 4, core: 2. Of those that a mesh axis runs over, the one named last changes fastest.
Arguments:
- queries: bfloat16 [256, 2048], P(('index', 'query')), may hold values from -4 to 4
- slab: bfloat16 [131072, 2048], P(('index', 'query')), may hold values from -24 to 24
- cand_owner: int32 [256, 32], P(('index', 'query')), may hold values from 0 to 31, all different within a row; in each aligned block of 8 rows (0 to 7, 8 to 15, ...) at most 8 rows name the same one
- cand_row: int32 [256, 32], P(('index', 'query')), may hold values from 0 to 4095
Outputs:
- pooled: float32 [256, 256], P(('index', 'query'))
- coarse_lse: float32 [256], P(('index', 'query'))
- margin: float32 [256, 32], P(('index', 'query'))
Inputs may be any that keep to these rules, and one draw needn't show every extreme that they name: `cand_owner`: each query names 32 distinct owners. Over the 8 queries of one device (aligned blocks of 8 rows) no owner is named more than 8 times, a bound that some block reaches.
All inputs are finite; a program needn't handle non-finite values.
Results may differ from a plain program's by a relative error of at most 0.00165.
Values may be sent and summed in bfloat16 or wider, within the bound.
No kernel may reach another device: no remote copies, remote signals or barrier semaphores. Data moves between devices by JAX's collectives and lax.ppermute only.
A program may use at most 128 MiB of HBM per device.

v0:
```python
import functools
import jax
import jax.numpy as jnp
from jax import lax
from jax.experimental import pallas as pl
from jax.experimental.pallas import tpu as pltpu
from jax.sharding import PartitionSpec as P

PREFIX = 256
AXES = ("index", "query")
RADIX = 64


def xor_stages(index_size, query_size):
    q_bits = query_size.bit_length() - 1
    i_bits = index_size.bit_length() - 1
    bits = [list(range(q_bits)), list(range(q_bits + 1, q_bits + i_bits)), [q_bits]]
    stages = []
    for group in bits:
        for at in range(0, len(group), 2):
            pair = group[at : at + 2]
            offs = [1 << pair[0]]
            if len(pair) == 2:
                offs += [1 << pair[1], (1 << pair[0]) | (1 << pair[1])]
            stages.append(offs)
    return stages


def swap(x, off, devices):
    return lax.ppermute(x, AXES, [(d, d ^ off) for d in range(devices)])


SMALL = pltpu.CompilerParams(vmem_limit_bytes=16 << 20)


def in_vmem(*arrays):
    return [pltpu.with_memory_space_constraint(a, pltpu.VMEM) for a in arrays]


def join_body(*refs):
    out_ref = refs[-1]
    at = 0
    for ref in refs[:-1]:
        out_ref[at : at + ref.shape[0], :] = ref[...]
        at += ref.shape[0]


def join(parts):
    rows = sum(p.shape[0] for p in parts)
    return pl.pallas_call(
        join_body, out_shape=pltpu.VMEM((rows, parts[0].shape[1]), parts[0].dtype), compiler_params=SMALL, name="join"
    )(*in_vmem(*parts))


def pack_body(q_ref, owner_ref, row_ref, out_ref, *, width, lanes, owners):
    out_ref[:, :width] = q_ref[...]
    lane = lax.broadcasted_iota(jnp.int32, (q_ref.shape[0], lanes), 1)
    table = jnp.zeros(lane.shape, jnp.int32)
    for k in range(owner_ref.shape[1]):
        own = owner_ref[:, k : k + 1]
        row = row_ref[:, k : k + 1] + 1
        table += jnp.where(lane == own, row // RADIX, 0)
        table += jnp.where(lane == own + owners, row % RADIX, 0)
    out_ref[:, width:] = table.astype(jnp.float32).astype(jnp.bfloat16)


def score_body(me_ref, x_ref, y_ref, slab_ref, keep_ref, send_ref, g_ref, rows_ref, logit_ref, sems, *, width, owners, chunk):
    r_dev = slab_ref.shape[0]
    n_q = g_ref.shape[0]
    half = n_q // 2
    g_ref[:half, :] = x_ref[...]
    g_ref[half:, :] = y_ref[...]
    n_chunks = r_dev // chunk
    scale = PREFIX ** (-0.5)

    def copy(c):
        at = pl.ds(c * chunk, chunk)
        return pltpu.make_async_copy(slab_ref.at[at], rows_ref.at[at], sems.at[c])

    @pl.when(pl.program_id(0) == 0)
    def _():
        for c in range(n_chunks):
            copy(c).start()

    me = me_ref[0]
    tab = g_ref[:, width:].astype(jnp.float32)
    lane = lax.broadcasted_iota(jnp.int32, tab.shape, 1)
    weight = jnp.where(lane == me, float(RADIX), 0.0) + jnp.where(lane == me + owners, 1.0, 0.0)
    want = jnp.sum(tab * weight, axis=1, keepdims=True).astype(jnp.int32) - 1

    best = jnp.full((n_q, 128), -jnp.inf, jnp.float32)
    score = jnp.zeros((n_q, 128), jnp.float32)
    contract = (((1,), (1,)), ((), ()))
    for c in range(n_chunks):
        at = slice(c * chunk, (c + 1) * chunk)

        @pl.when(pl.program_id(0) == 0)
        def _():
            copy(c).wait()

        logits = lax.dot_general(
            g_ref[:, :PREFIX], rows_ref[at, :PREFIX], contract, preferred_element_type=jnp.float32
        )
        logit_ref[:, at] = logits
        full = lax.dot_general(
            g_ref[:, PREFIX:width], rows_ref[at, PREFIX:], contract, preferred_element_type=jnp.float32
        )
        full = full + logits
        col = lax.broadcasted_iota(jnp.int32, (n_q, 128), 1)
        for s in range(chunk // 128):
            part = slice(s * 128, (s + 1) * 128)
            best = jnp.maximum(best, logits[:, part])
            score += jnp.where(col + (c * chunk + s * 128) == want, full[:, part], 0.0)
    top = jnp.max(best, axis=1, keepdims=True)
    score = jnp.sum(score, axis=1, keepdims=True) * width ** (-0.5)
    acc = jnp.zeros((n_q, PREFIX), jnp.float32)
    total = jnp.zeros((n_q, 128), jnp.float32)
    for c in range(n_chunks):
        at = slice(c * chunk, (c + 1) * chunk)
        weights = jnp.exp((logit_ref[:, at] - top) * scale)
        for s in range(chunk // 128):
            total += weights[:, s * 128 : (s + 1) * 128]
        acc += jnp.dot(
            weights.astype(jnp.bfloat16), rows_ref[at, :PREFIX], preferred_element_type=jnp.float32
        )
    total = jnp.sum(total, axis=1, keepdims=True)
    tail = keep_ref.shape[1] - PREFIX
    lane = lax.broadcasted_iota(jnp.int32, (n_q, tail), 1)
    rest = jnp.where(
        lane == tail - 1, top * scale, jnp.where(lane == tail - 2, total, jnp.where(lane == me, score, 0.0))
    )
    keep_ref[:, :PREFIX] = acc[:half, :]
    keep_ref[:, PREFIX:] = rest[:half, :]
    send_ref[:, :PREFIX] = acc[half:, :]
    send_ref[:, PREFIX:] = rest[half:, :]


def merge(parts):
    wide = parts[0].shape[1]
    tops = [p[:, wide - 1 :] for p in parts]
    top = functools.reduce(jnp.maximum, tops)
    lane = lax.broadcasted_iota(jnp.int32, parts[0].shape, 1)
    scaled = (lane < PREFIX) | (lane == wide - 2)
    out = jnp.zeros(parts[0].shape, jnp.float32)
    for part, t in zip(parts, tops):
        out += part * jnp.where(scaled, jnp.exp(t - top), 1.0)
    return jnp.where(lane == wide - 1, top, out)


def merge_body(*refs, n_parts):
    out = merge([r[...] for r in refs[:n_parts]])
    at = 0
    for ref in refs[n_parts:]:
        ref[...] = out[at : at + ref.shape[0], :]
        at += ref.shape[0]


def finish_body(owner_ref, *refs, owners):
    parts, (pooled_ref, lse_ref, margin_ref) = refs[:-3], refs[-3:]
    out = merge([r[...] for r in parts])
    wide = out.shape[1]
    total = out[:, wide - 2 : wide - 1]
    lse = out[:, wide - 1 :] + jnp.log(total)
    pooled_ref[...] = out[:, :PREFIX] / total
    n = lse.shape[0]
    square = (n, n)
    eye = lax.broadcasted_iota(jnp.int32, square, 0) == lax.broadcasted_iota(jnp.int32, square, 1)
    lse_ref[...] = jnp.sum(jnp.where(eye, lse, 0.0), axis=0, keepdims=True)
    own = owner_ref[...]
    full = jnp.zeros(own.shape, jnp.float32)
    for o in range(owners):
        full += jnp.where(own == o, out[:, PREFIX + o : PREFIX + o + 1], 0.0)
    margin_ref[...] = full - lse


def on_device(queries, slab, cand_owner, cand_row, *, index_size, query_size):
    devices = index_size * query_size
    q_dev, width = queries.shape
    owners = devices
    stages = xor_stages(index_size, query_size)
    lanes = -(-2 * owners // 128) * 128
    tail = -(-(owners + 2) // 128) * 128
    me = lax.axis_index(AXES).astype(jnp.int32).reshape(1)
    f32 = jnp.float32

    x = pl.pallas_call(
        functools.partial(pack_body, width=width, lanes=lanes, owners=owners),
        out_shape=pltpu.VMEM((q_dev, width + lanes), jnp.bfloat16),
        compiler_params=SMALL,
        name="pack",
    )(queries, cand_owner, cand_row)
    for offs in stages[:-1]:
        x = join([x] + [swap(x, off, devices) for off in offs])
    y = swap(x, stages[-1][0], devices)

    n_half = x.shape[0]
    half = min(n_half, 128)
    wide = PREFIX + tail
    r_dev = slab.shape[0]
    chunk = 512
    pair = [pl.BlockSpec((half, width + lanes), lambda i: (i, 0))] * 2
    if n_half == half:
        pair = [pl.BlockSpec(memory_space=pltpu.VMEM)] * 2
        x, y = in_vmem(x, y)
        outs = [pl.BlockSpec(memory_space=pltpu.VMEM)] * 2
        shape = pltpu.VMEM((n_half, wide), f32)
    else:
        outs = [pl.BlockSpec((half, wide), lambda i: (i, 0))] * 2
        shape = jax.ShapeDtypeStruct((n_half, wide), f32)
    keep, send = pl.pallas_call(
        functools.partial(score_body, width=width, owners=owners, chunk=chunk),
        grid=(n_half // half,),
        in_specs=[pl.BlockSpec(memory_space=pltpu.SMEM), *pair, pl.BlockSpec(memory_space=pl.ANY)],
        out_specs=outs,
        out_shape=(shape, shape),
        scratch_shapes=[
            pltpu.VMEM((2 * half, width + lanes), jnp.bfloat16),
            pltpu.VMEM((r_dev, width), jnp.bfloat16),
            pltpu.VMEM((2 * half, r_dev), f32),
            pltpu.SemaphoreType.DMA((r_dev // chunk,)),
        ],
        compiler_params=pltpu.CompilerParams(vmem_limit_bytes=36000 * 1024),
        name="score",
    )(me, x, y, slab)

    parts = [keep, swap(send, stages[-1][0], devices)]
    for offs in reversed(stages[:-1]):
        n = parts[0].shape[0] // (len(offs) + 1)
        keep, *sends = pl.pallas_call(
            functools.partial(merge_body, n_parts=len(parts)),
            out_shape=tuple(pltpu.VMEM((n, wide), f32) for _ in range(len(offs) + 1)),
            compiler_params=SMALL,
            name="merge",
        )(*in_vmem(*parts))
        parts = [keep] + [swap(s, off, devices) for s, off in zip(sends, offs)]
    pooled, lse, margin = pl.pallas_call(
        functools.partial(finish_body, owners=owners),
        out_shape=(
            jax.ShapeDtypeStruct((q_dev, PREFIX), f32),
            jax.ShapeDtypeStruct((1, q_dev), f32),
            jax.ShapeDtypeStruct(cand_owner.shape, f32),
        ),
        compiler_params=SMALL,
        name="finish",
    )(cand_owner, *in_vmem(*parts))
    return pooled, lse.reshape(q_dev), margin


def solution(mesh):
    spec = P(AXES, None)
    body = functools.partial(
        on_device, index_size=mesh.shape["index"], query_size=mesh.shape["query"]
    )
    return jax.shard_map(
        body,
        mesh=mesh,
        in_specs=(spec, spec, spec, spec),
        out_specs=(spec, P(AXES), spec),
        check_vma=False,
    )
```

profile of v0, /device:TPU:0, one launch (start us, length us, event | category | flops | bytes accessed | tf_op | source)
XLA Modules:
  0.0 56.5 jit_solution(1806256580635574673)
XLA Ops:
  0.6 0.7 %copy-done.1 = bf16[8,2048]{1,0:T(8,128)(2,1)S(1)} copy-done((bf16[8,2048]{1,0:T(8,128)(2,1)S(1)}, bf16[8,2048]{1,0:T(8,128)(2,1)}, u32[]{:S(2)}) %copy-start.1) | copy-done | bytes 32792
  1.4 0.7 %copy-done.2 = s32[8,32]{1,0:T(8,128)S(1)} copy-done((s32[8,32]{1,0:T(8,128)S(1)}, s32[8,32]{1,0:T(8,128)}, u32[]{:S(2)}) %copy-start.2) | copy-done | bytes 1048
  2.1 0.7 %copy-done.4 = s32[8,32]{1,0:T(8,128)S(1)} copy-done((s32[8,32]{1,0:T(8,128)S(1)}, s32[8,32]{1,0:T(8,128)}, u32[]{:S(2)}) %copy-start.4) | copy-done | bytes 1048
  2.8 0.3 pack.1.refs_0_
  3.0 5.1 %collective-permute-start.2 = (bf16[8,2176]{1,0:T(8,128)(2,1)S(1)}, bf16[8,2176]{1,0:T(8,128)(2,1)S(1)}, u32[]{:S(2)}, u32[]{:S(2)}) collective-permute-start(bf16[8,2176]{1,0:T(8,128)(2,1)S(1)} %pack.1.refs_0_), channel_id=1, source_target_pairs={{0,3},{1,2},{2,1},{3,0},{4,7},{5,6},{6,5},{7,4},{8,11},{9,10},{10,... | collective-permute-start | bytes 104456 | tf_op jit(solution)/shard_map/ppermute | solution.py:30
  8.2 0.6 %collective-permute-start = (bf16[8,2176]{1,0:T(8,128)(2,1)S(1)}, bf16[8,2176]{1,0:T(8,128)(2,1)S(1)}, u32[]{:S(2)}, u32[]{:S(2)}) collective-permute-start(bf16[8,2176]{1,0:T(8,128)(2,1)S(1)} %pack.1.refs_0_), channel_id=1, source_target_pairs={{0,1},{1,0},{2,3},{3,2},{4,5},{5,4},{6,7},{7,6},{8,9},{9,8},{10,11... | collective-permute-start | bytes 104456 | tf_op jit(solution)/shard_map/ppermute | solution.py:30
  8.8 1.3 %collective-permute-done.2.refs_3_ = bf16[8,2176]{1,0:T(8,128)(2,1)S(1)} collective-permute-done((bf16[8,2176]{1,0:T(8,128)(2,1)S(1)}, bf16[8,2176]{1,0:T(8,128)(2,1)S(1)}, u32[]{:S(2)}, u32[]{:S(2)}) %collective-permute-start.2) | collective-permute-done | bytes 34848 | tf_op jit(solution)/shard_map/ppermute | solution.py:30
  10.1 2.9 %collective-permute-done.1.refs_2_ = bf16[8,2176]{1,0:T(8,128)(2,1)S(1)} collective-permute-done((bf16[8,2176]{1,0:T(8,128)(2,1)S(1)}, bf16[8,2176]{1,0:T(8,128)(2,1)S(1)}, u32[]{:S(2)}, u32[]{:S(2)}) %collective-permute-start.1) | collective-permute-done | bytes 34848 | tf_op jit(solution)/shard_map/ppermute | solution.py:30
  13.0 2.5 %collective-permute-start.5 = (bf16[32,2176]{1,0:T(8,128)(2,1)S(1)}, bf16[32,2176]{1,0:T(8,128)(2,1)S(1)}, u32[]{:S(2)}, u32[]{:S(2)}) collective-permute-start(bf16[32,2176]{1,0:T(8,128)(2,1)S(1)} %join.2.refs_0_), channel_id=1, source_target_pairs={{0,24},{1,25},{2,26},{3,27},{4,28},{5,29},{6,30},{7,31},{8,16},{9,... | collective-permute-start | bytes 417800 | tf_op jit(solution)/shard_map/ppermute | solution.py:30
  15.5 0.5 collective-permute-start.4
  16.0 0.5 collective-permute-start.3
  16.6 3.9 %collective-permute-done.5.refs_3_ = bf16[32,2176]{1,0:T(8,128)(2,1)S(1)} collective-permute-done((bf16[32,2176]{1,0:T(8,128)(2,1)S(1)}, bf16[32,2176]{1,0:T(8,128)(2,1)S(1)}, u32[]{:S(2)}, u32[]{:S(2)}) %collective-permute-start.5) | collective-permute-done | bytes 139296 | tf_op jit(solution)/shard_map/ppermute | solution.py:30
  20.5 0.8 %collective-permute-done.4.refs_2_ = bf16[32,2176]{1,0:T(8,128)(2,1)S(1)} collective-permute-done((bf16[32,2176]{1,0:T(8,128)(2,1)S(1)}, bf16[32,2176]{1,0:T(8,128)(2,1)S(1)}, u32[]{:S(2)}, u32[]{:S(2)}) %collective-permute-start.4) | collective-permute-done | bytes 139296 | tf_op jit(solution)/shard_map/ppermute | solution.py:30
  21.4 1.9 %collective-permute-done.6.y_ref = bf16[128,2176]{1,0:T(8,128)(2,1)S(1)} collective-permute-done((bf16[128,2176]{1,0:T(8,128)(2,1)S(1)}, bf16[128,2176]{1,0:T(8,128)(2,1)S(1)}, u32[]{:S(2)}, u32[]{:S(2)}) %collective-permute-start.6) | collective-permute-done | bytes 557088 | tf_op jit(solution)/shard_map/ppermute | solution.py:30
  23.4 5.8 %copy-done = bf16[4096,2048]{1,0:T(8,128)(2,1)S(1)} copy-done((bf16[4096,2048]{1,0:T(8,128)(2,1)S(1)}, bf16[4096,2048]{1,0:T(8,128)(2,1)}, u32[]{:S(2)}) %copy-start) | copy-done | bytes 16777240
  29.1 9.7 %score.1 = (f32[128,384]{1,0:T(8,128)S(1)}, f32[128,384]{1,0:T(8,128)S(1)}) custom-call(s32[1]{0:T(128)} %bitcast.me_ref, bf16[128,2176]{1,0:T(8,128)(2,1)S(1)} %join.3.x_ref, bf16[128,2176]{1,0:T(8,128)(2,1)S(1)} %collective-permute-done.6.y_ref, bf16[4096,2048]{1,0:T(8,128)(2,1)S(1)} %copy-done), custom_call_target="tpu_custom_call" | custom-call | tf_op jit(solution)/shard_map/score/pallas_call | solution.py:210
  38.9 0.2 collective-permute-start.7
  39.1 1.3 %collective-permute-done.7.refs_1_ = f32[128,384]{1,0:T(8,128)S(1)} collective-permute-done((f32[128,384]{1,0:T(8,128)S(1)}, f32[128,384]{1,0:T(8,128)S(1)}, u32[]{:S(2)}, u32[]{:S(2)}) %collective-permute-start.7) | collective-permute-done | bytes 196640 | tf_op jit(solution)/shard_map/ppermute | solution.py:30
  40.4 0.1 merge.2
  40.5 1.3 %collective-permute-start.8 = (f32[32,384]{1,0:T(8,128)S(1)}, f32[32,384]{1,0:T(8,128)S(1)}, u32[]{:S(2)}, u32[]{:S(2)}) collective-permute-start(f32[32,384]{1,0:T(8,128)S(1)} %get-tuple-element.19), channel_id=1, source_target_pairs={{0,8},{1,9},{2,10},{3,11},{4,12},{5,13},{6,14},{7,15},{8,0},{9,1},... | collective-permute-start | bytes 147464 | tf_op jit(solution)/shard_map/ppermute | solution.py:30
  41.9 0.7 %collective-permute-start.9 = (f32[32,384]{1,0:T(8,128)S(1)}, f32[32,384]{1,0:T(8,128)S(1)}, u32[]{:S(2)}, u32[]{:S(2)}) collective-permute-start(f32[32,384]{1,0:T(8,128)S(1)} %get-tuple-element.20), channel_id=1, source_target_pairs={{0,16},{1,17},{2,18},{3,19},{4,20},{5,21},{6,22},{7,23},{8,24},{9,... | collective-permute-start | bytes 147464 | tf_op jit(solution)/shard_map/ppermute | solution.py:30
  42.5 1.5 %collective-permute-start.10 = (f32[32,384]{1,0:T(8,128)S(1)}, f32[32,384]{1,0:T(8,128)S(1)}, u32[]{:S(2)}, u32[]{:S(2)}) collective-permute-start(f32[32,384]{1,0:T(8,128)S(1)} %get-tuple-element.21), channel_id=1, source_target_pairs={{0,24},{1,25},{2,26},{3,27},{4,28},{5,29},{6,30},{7,31},{8,16},{9,... | collective-permute-start | bytes 147464 | tf_op jit(solution)/shard_map/ppermute | solution.py:30
  44.1 0.6 %collective-permute-done.8.refs_1_ = f32[32,384]{1,0:T(8,128)S(1)} collective-permute-done((f32[32,384]{1,0:T(8,128)S(1)}, f32[32,384]{1,0:T(8,128)S(1)}, u32[]{:S(2)}, u32[]{:S(2)}) %collective-permute-start.8) | collective-permute-done | bytes 49184 | tf_op jit(solution)/shard_map/ppermute | solution.py:30
  44.7 1.8 %collective-permute-done.9.refs_2_ = f32[32,384]{1,0:T(8,128)S(1)} collective-permute-done((f32[32,384]{1,0:T(8,128)S(1)}, f32[32,384]{1,0:T(8,128)S(1)}, u32[]{:S(2)}, u32[]{:S(2)}) %collective-permute-start.9) | collective-permute-done | bytes 49184 | tf_op jit(solution)/shard_map/ppermute | solution.py:30
  46.5 1.0 %collective-permute-done.10.refs_3_ = f32[32,384]{1,0:T(8,128)S(1)} collective-permute-done((f32[32,384]{1,0:T(8,128)S(1)}, f32[32,384]{1,0:T(8,128)S(1)}, u32[]{:S(2)}, u32[]{:S(2)}) %collective-permute-start.10) | collective-permute-done | bytes 49184 | tf_op jit(solution)/shard_map/ppermute | solution.py:30
  47.5 0.1 merge.3
  47.6 0.2 collective-permute-start.11
  47.8 2.3 %collective-permute-start.12 = (f32[8,384]{1,0:T(8,128)S(1)}, f32[8,384]{1,0:T(8,128)S(1)}, u32[]{:S(2)}, u32[]{:S(2)}) collective-permute-start(f32[8,384]{1,0:T(8,128)S(1)} %get-tuple-element.24), channel_id=1, source_target_pairs={{0,2},{1,3},{2,0},{3,1},{4,6},{5,7},{6,4},{7,5},{8,10},{9,11},{10,... | collective-permute-start | bytes 36872 | tf_op jit(solution)/shard_map/ppermute | solution.py:30
  50.2 1.9 %collective-permute-start.13 = (f32[8,384]{1,0:T(8,128)S(1)}, f32[8,384]{1,0:T(8,128)S(1)}, u32[]{:S(2)}, u32[]{:S(2)}) collective-permute-start(f32[8,384]{1,0:T(8,128)S(1)} %get-tuple-element.25), channel_id=1, source_target_pairs={{0,3},{1,2},{2,1},{3,0},{4,7},{5,6},{6,5},{7,4},{8,11},{9,10},{10,... | collective-permute-start | bytes 36872 | tf_op jit(solution)/shard_map/ppermute | solution.py:30
  52.1 0.3 collective-permute-done.12.refs_2_
  52.4 3.2 %collective-permute-done.13.refs_3_ = f32[8,384]{1,0:T(8,128)S(1)} collective-permute-done((f32[8,384]{1,0:T(8,128)S(1)}, f32[8,384]{1,0:T(8,128)S(1)}, u32[]{:S(2)}, u32[]{:S(2)}) %collective-permute-start.13) | collective-permute-done | bytes 12320 | tf_op jit(solution)/shard_map/ppermute | solution.py:30
  55.6 0.8 %finish.1 = (f32[8,256]{1,0:T(8,128)}, f32[1,8]{1,0:T(1,128)}, f32[8,32]{1,0:T(8,128)}) custom-call(s32[8,32]{1,0:T(8,128)S(1)} %copy-done.3, f32[8,384]{1,0:T(8,128)S(1)} %get-tuple-element.22.refs_0_, f32[8,384]{1,0:T(8,128)S(1)} %collective-permute-done.11.refs_1_, f32[8,384]{1,0:T(8,128)S(1)} %collective-permute-done.12.refs_2_, ...), custom_call_target="tpu_custom_call" | custom-call | tf_op jit(solution)/shard_map/finish/pallas_call | solution.py:236
  (13 shorter events, 0.1 us)
Async XLA Ops:
  0.6 0.8 %copy-start.1 = (bf16[8,2048]{1,0:T(8,128)(2,1)S(1)}, bf16[8,2048]{1,0:T(8,128)(2,1)}, u32[]{:S(2)}) copy-start(bf16[8,2048]{1,0:T(8,128)(2,1)} %q_ref.1) | copy-start | bytes 98308
  1.4 0.7 %copy-start.2 = (s32[8,32]{1,0:T(8,128)S(1)}, s32[8,32]{1,0:T(8,128)}, u32[]{:S(2)}) copy-start(s32[8,32]{1,0:T(8,128)} %owner_ref.3) | copy-start | bytes 3076
  2.1 0.7 %copy-start.4 = (s32[8,32]{1,0:T(8,128)S(1)}, s32[8,32]{1,0:T(8,128)}, u32[]{:S(2)}) copy-start(s32[8,32]{1,0:T(8,128)} %row_ref.1) | copy-start | bytes 3076
  2.8 52.9 %copy-start.3 = (s32[8,32]{1,0:T(8,128)S(1)}, s32[8,32]{1,0:T(8,128)}, u32[]{:S(2)}) copy-start(s32[8,32]{1,0:T(8,128)} %owner_ref.3) | copy-start | bytes 3076
  3.0 7.1 %collective-permute-start.2 = (bf16[8,2176]{1,0:T(8,128)(2,1)S(1)}, bf16[8,2176]{1,0:T(8,128)(2,1)S(1)}, u32[]{:S(2)}, u32[]{:S(2)}) collective-permute-start(bf16[8,2176]{1,0:T(8,128)(2,1)S(1)} %pack.1.refs_0_), channel_id=1, source_target_pairs={{0,3},{1,2},{2,1},{3,0},{4,7},{5,6},{6,5},{7,4},{8,11},{9,10},{10,... | collective-permute-start | bytes 104456 | tf_op jit(solution)/shard_map/ppermute | solution.py:30
  8.2 4.8 %collective-permute-start.1 = (bf16[8,2176]{1,0:T(8,128)(2,1)S(1)}, bf16[8,2176]{1,0:T(8,128)(2,1)S(1)}, u32[]{:S(2)}, u32[]{:S(2)}) collective-permute-start(bf16[8,2176]{1,0:T(8,128)(2,1)S(1)} %pack.1.refs_0_), channel_id=1, source_target_pairs={{0,2},{1,3},{2,0},{3,1},{4,6},{5,7},{6,4},{7,5},{8,10},{9,11},{10,... | collective-permute-start | bytes 104456 | tf_op jit(solution)/shard_map/ppermute | solution.py:30
  8.2 4.8 %collective-permute-start = (bf16[8,2176]{1,0:T(8,128)(2,1)S(1)}, bf16[8,2176]{1,0:T(8,128)(2,1)S(1)}, u32[]{:S(2)}, u32[]{:S(2)}) collective-permute-start(bf16[8,2176]{1,0:T(8,128)(2,1)S(1)} %pack.1.refs_0_), channel_id=1, source_target_pairs={{0,1},{1,0},{2,3},{3,2},{4,5},{5,4},{6,7},{7,6},{8,9},{9,8},{10,11... | collective-permute-start | bytes 104456 | tf_op jit(solution)/shard_map/ppermute | solution.py:30
  13.0 7.5 %collective-permute-start.5 = (bf16[32,2176]{1,0:T(8,128)(2,1)S(1)}, bf16[32,2176]{1,0:T(8,128)(2,1)S(1)}, u32[]{:S(2)}, u32[]{:S(2)}) collective-permute-start(bf16[32,2176]{1,0:T(8,128)(2,1)S(1)} %join.2.refs_0_), channel_id=1, source_target_pairs={{0,24},{1,25},{2,26},{3,27},{4,28},{5,29},{6,30},{7,31},{8,16},{9,... | collective-permute-start | bytes 417800 | tf_op jit(solution)/shard_map/ppermute | solution.py:30
  15.5 5.8 %collective-permute-start.4 = (bf16[32,2176]{1,0:T(8,128)(2,1)S(1)}, bf16[32,2176]{1,0:T(8,128)(2,1)S(1)}, u32[]{:S(2)}, u32[]{:S(2)}) collective-permute-start(bf16[32,2176]{1,0:T(8,128)(2,1)S(1)} %join.2.refs_0_), channel_id=1, source_target_pairs={{0,16},{1,17},{2,18},{3,19},{4,20},{5,21},{6,22},{7,23},{8,24},{9,... | collective-permute-start | bytes 417800 | tf_op jit(solution)/shard_map/ppermute | solution.py:30
  16.0 5.3 %collective-permute-start.3 = (bf16[32,2176]{1,0:T(8,128)(2,1)S(1)}, bf16[32,2176]{1,0:T(8,128)(2,1)S(1)}, u32[]{:S(2)}, u32[]{:S(2)}) collective-permute-start(bf16[32,2176]{1,0:T(8,128)(2,1)S(1)} %join.2.refs_0_), channel_id=1, source_target_pairs={{0,8},{1,9},{2,10},{3,11},{4,12},{5,13},{6,14},{7,15},{8,0},{9,1},... | collective-permute-start | bytes 417800 | tf_op jit(solution)/shard_map/ppermute | solution.py:30
  21.4 2.0 %collective-permute-start.6 = (bf16[128,2176]{1,0:T(8,128)(2,1)S(1)}, bf16[128,2176]{1,0:T(8,128)(2,1)S(1)}, u32[]{:S(2)}, u32[]{:S(2)}) collective-permute-start(bf16[128,2176]{1,0:T(8,128)(2,1)S(1)} %join.3.x_ref), channel_id=1, source_target_pairs={{0,4},{1,5},{2,6},{3,7},{4,0},{5,1},{6,2},{7,3},{8,12},{9,13},{10,... | collective-permute-start | bytes 1671176 | tf_op jit(solution)/shard_map/ppermute | solution.py:30
  23.4 5.8 %copy-start = (bf16[4096,2048]{1,0:T(8,128)(2,1)S(1)}, bf16[4096,2048]{1,0:T(8,128)(2,1)}, u32[]{:S(2)}) copy-start(bf16[4096,2048]{1,0:T(8,128)(2,1)} %slab_ref.1) | copy-start | bytes 50331652
  38.9 1.5 %collective-permute-start.7 = (f32[128,384]{1,0:T(8,128)S(1)}, f32[128,384]{1,0:T(8,128)S(1)}, u32[]{:S(2)}, u32[]{:S(2)}) collective-permute-start(f32[128,384]{1,0:T(8,128)S(1)} %get-tuple-element.17), channel_id=1, source_target_pairs={{0,4},{1,5},{2,6},{3,7},{4,0},{5,1},{6,2},{7,3},{8,12},{9,13},{10,... | collective-permute-start | bytes 589832 | tf_op jit(solution)/shard_map/ppermute | solution.py:30
  40.5 4.2 %collective-permute-start.8 = (f32[32,384]{1,0:T(8,128)S(1)}, f32[32,384]{1,0:T(8,128)S(1)}, u32[]{:S(2)}, u32[]{:S(2)}) collective-permute-start(f32[32,384]{1,0:T(8,128)S(1)} %get-tuple-element.19), channel_id=1, source_target_pairs={{0,8},{1,9},{2,10},{3,11},{4,12},{5,13},{6,14},{7,15},{8,0},{9,1},... | collective-permute-start | bytes 147464 | tf_op jit(solution)/shard_map/ppermute | solution.py:30
  41.9 4.6 %collective-permute-start.9 = (f32[32,384]{1,0:T(8,128)S(1)}, f32[32,384]{1,0:T(8,128)S(1)}, u32[]{:S(2)}, u32[]{:S(2)}) collective-permute-start(f32[32,384]{1,0:T(8,128)S(1)} %get-tuple-element.20), channel_id=1, source_target_pairs={{0,16},{1,17},{2,18},{3,19},{4,20},{5,21},{6,22},{7,23},{8,24},{9,... | collective-permute-start | bytes 147464 | tf_op jit(solution)/shard_map/ppermute | solution.py:30
  42.5 5.0 %collective-permute-start.10 = (f32[32,384]{1,0:T(8,128)S(1)}, f32[32,384]{1,0:T(8,128)S(1)}, u32[]{:S(2)}, u32[]{:S(2)}) collective-permute-start(f32[32,384]{1,0:T(8,128)S(1)} %get-tuple-element.21), channel_id=1, source_target_pairs={{0,24},{1,25},{2,26},{3,27},{4,28},{5,29},{6,30},{7,31},{8,16},{9,... | collective-permute-start | bytes 147464 | tf_op jit(solution)/shard_map/ppermute | solution.py:30
  47.6 4.5 %collective-permute-start.11 = (f32[8,384]{1,0:T(8,128)S(1)}, f32[8,384]{1,0:T(8,128)S(1)}, u32[]{:S(2)}, u32[]{:S(2)}) collective-permute-start(f32[8,384]{1,0:T(8,128)S(1)} %get-tuple-element.23), channel_id=1, source_target_pairs={{0,1},{1,0},{2,3},{3,2},{4,5},{5,4},{6,7},{7,6},{8,9},{9,8},{10,11... | collective-permute-start | bytes 36872 | tf_op jit(solution)/shard_map/ppermute | solution.py:30
  47.8 4.6 %collective-permute-start.12 = (f32[8,384]{1,0:T(8,128)S(1)}, f32[8,384]{1,0:T(8,128)S(1)}, u32[]{:S(2)}, u32[]{:S(2)}) collective-permute-start(f32[8,384]{1,0:T(8,128)S(1)} %get-tuple-element.24), channel_id=1, source_target_pairs={{0,2},{1,3},{2,0},{3,1},{4,6},{5,7},{6,4},{7,5},{8,10},{9,11},{10,... | collective-permute-start | bytes 36872 | tf_op jit(solution)/shard_map/ppermute | solution.py:30
  50.2 5.5 %collective-permute-start.13 = (f32[8,384]{1,0:T(8,128)S(1)}, f32[8,384]{1,0:T(8,128)S(1)}, u32[]{:S(2)}, u32[]{:S(2)}) collective-permute-start(f32[8,384]{1,0:T(8,128)S(1)} %get-tuple-element.25), channel_id=1, source_target_pairs={{0,3},{1,2},{2,1},{3,0},{4,7},{5,6},{6,5},{7,4},{8,11},{9,10},{10,... | collective-permute-start | bytes 36872 | tf_op jit(solution)/shard_map/ppermute | solution.py:30
where the time goes:
time: 56.8 us; the launch traced here: 56.5 us
  waiting for transfers between devices  19.2 us (34%)
  starting transfers between devices  17.6 us (31%)
  Pallas kernels  11.1 us (20%)
  local copies, waits for them, and re-layouts  7.9 us (14%)
  between operations  0.71 us (1%)
    ppermute x14, waiting for transfers between devices, swap(): return lax.ppermute(x, AXES, [(d, d ^ off) for d in range(devices)])  19.2 us
    ppermute x14, starting transfers between devices, swap(): return lax.ppermute(x, AXES, [(d, d ^ off) for d in range(devices)])  17.6 us
    pallas_call x1, Pallas kernels, on_device(): pl.pallas_call(functools.partial(score_body, width=width, owners=owners,...  9.72 us
    unnamed x10, local copies, waits for them, and re-layouts  7.9 us
  transfers between devices with their start and end apart: 14, of which 11 were waited for; matrix products, arithmetic and copies ran while one was open for 0% of the time, Pallas kernels for 0%

commit v1 on v0

--- a/solution.py
+++ b/solution.py
@@ -5,6 +5,7 @@
 from jax.experimental import pallas as pl
 from jax.experimental.pallas import tpu as pltpu
 from jax.sharding import PartitionSpec as P
+
 
 PREFIX = 256
 AXES = ("index", "query")
@@ -37,6 +38,10 @@
     return [pltpu.with_memory_space_constraint(a, pltpu.VMEM) for a in arrays]
 
 
+def in_hbm(*arrays):
+    return [pltpu.with_memory_space_constraint(a, pltpu.HBM) for a in arrays]
+
+
 def join_body(*refs):
     out_ref = refs[-1]
     at = 0
@@ -52,9 +57,38 @@
     )(*in_vmem(*parts))
 
 
-def pack_body(q_ref, owner_ref, row_ref, out_ref, *, width, lanes, owners):
-    out_ref[:, :width] = q_ref[...]
-    lane = lax.broadcasted_iota(jnp.int32, (q_ref.shape[0], lanes), 1)
+def load_body(from_ref, out_ref, sem, *, first):
+    rows = out_ref.shape[0]
+    copy = pltpu.make_async_copy(from_ref.at[pl.ds(first, rows)], out_ref, sem)
+    copy.start()
+    copy.wait()
+
+
+def load(slab, first, rows):
+    return pl.pallas_call(
+        functools.partial(load_body, first=first),
+        in_specs=[pl.BlockSpec(memory_space=pltpu.HBM)],
+        out_shape=pltpu.VMEM((rows, slab.shape[1]), slab.dtype),
+        scratch_shapes=[pltpu.SemaphoreType.DMA],
+        compiler_params=SMALL,
+        cost_estimate=pl.CostEstimate(
+            flops=0, transcendentals=0, bytes_accessed=2 * rows * slab.shape[1]
+        ),
+        name="load",
+    )(*in_hbm(slab))
+
+
+def pack_body(q_hbm, owner_hbm, row_hbm, out_ref, owner_ref, row_ref, sems, *, width, lanes, owners):
+    copies = [
+        pltpu.make_async_copy(owner_hbm, owner_ref, sems.at[0]),
+        pltpu.make_async_copy(row_hbm, row_ref, sems.at[1]),
+        pltpu.make_async_copy(q_hbm, out_ref.at[:, pl.ds(0, width)], sems.at[2]),
+    ]
+    for copy in copies:
+        copy.start()
+    copies[0].wait()
+    copies[1].wait()
+    lane = lax.broadcasted_iota(jnp.int32, (owner_ref.shape[0], lanes), 1)
     table = jnp.zeros(lane.shape, jnp.int32)
     for k in range(owner_ref.shape[1]):
         own = owner_ref[:, k : k + 1]
@@ -62,27 +96,23 @@
         table += jnp.where(lane == own, row // RADIX, 0)
         table += jnp.where(lane == own + owners, row % RADIX, 0)
     out_ref[:, width:] = table.astype(jnp.float32).astype(jnp.bfloat16)
-
-
-def score_body(me_ref, x_ref, y_ref, slab_ref, keep_ref, send_ref, g_ref, rows_ref, logit_ref, sems, *, width, owners, chunk):
-    r_dev = slab_ref.shape[0]
+    copies[2].wait()
+
+
+def score_body(x_ref, y_ref, rows_a, rows_b, rows_c, keep_ref, send_ref, g_ref, logit_ref, *, width, owners, chunk):
+    rows = [
+        (ref, slice(at, at + chunk))
+        for ref in (rows_a, rows_b, rows_c)
+        for at in range(0, ref.shape[0], chunk)
+    ]
     n_q = g_ref.shape[0]
     half = n_q // 2
     g_ref[:half, :] = x_ref[...]
     g_ref[half:, :] = y_ref[...]
-    n_chunks = r_dev // chunk
+    n_chunks = len(rows)
     scale = PREFIX ** (-0.5)
 
-    def copy(c):
-        at = pl.ds(c * chunk, chunk)
-        return pltpu.make_async_copy(slab_ref.at[at], rows_ref.at[at], sems.at[c])
-
-    @pl.when(pl.program_id(0) == 0)
-    def _():
-        for c in range(n_chunks):
-            copy(c).start()
-
-    me = me_ref[0]
+    me = lax.axis_index("index") * lax.axis_size("query") + lax.axis_index("query")
     tab = g_ref[:, width:].astype(jnp.float32)
     lane = lax.broadcasted_iota(jnp.int32, tab.shape, 1)
     weight = jnp.where(lane == me, float(RADIX), 0.0) + jnp.where(lane == me + owners, 1.0, 0.0)
@@ -93,17 +123,13 @@
     contract = (((1,), (1,)), ((), ()))
     for c in range(n_chunks):
         at = slice(c * chunk, (c + 1) * chunk)
-
-        @pl.when(pl.program_id(0) == 0)
-        def _():
-            copy(c).wait()
-
+        ref, own = rows[c]
         logits = lax.dot_general(
-            g_ref[:, :PREFIX], rows_ref[at, :PREFIX], contract, preferred_element_type=jnp.float32
+            g_ref[:, :PREFIX], ref[own, :PREFIX], contract, preferred_element_type=jnp.float32
         )
         logit_ref[:, at] = logits
         full = lax.dot_general(
-            g_ref[:, PREFIX:width], rows_ref[at, PREFIX:], contract, preferred_element_type=jnp.float32
+            g_ref[:, PREFIX:width], ref[own, PREFIX:], contract, preferred_element_type=jnp.float32
         )
         full = full + logits
         col = lax.broadcasted_iota(jnp.int32, (n_q, 128), 1)
@@ -117,11 +143,12 @@
     total = jnp.zeros((n_q, 128), jnp.float32)
     for c in range(n_chunks):
         at = slice(c * chunk, (c + 1) * chunk)
+        ref, own = rows[c]
         weights = jnp.exp((logit_ref[:, at] - top) * scale)
         for s in range(chunk // 128):
             total += weights[:, s * 128 : (s + 1) * 128]
         acc += jnp.dot(
-            weights.astype(jnp.bfloat16), rows_ref[at, :PREFIX], preferred_element_type=jnp.float32
+            weights.astype(jnp.bfloat16), ref[own, :PREFIX], preferred_element_type=jnp.float32
         )
     total = jnp.sum(total, axis=1, keepdims=True)
     tail = keep_ref.shape[1] - PREFIX
@@ -180,24 +207,36 @@
     stages = xor_stages(index_size, query_size)
     lanes = -(-2 * owners // 128) * 128
     tail = -(-(owners + 2) // 128) * 128
-    me = lax.axis_index(AXES).astype(jnp.int32).reshape(1)
     f32 = jnp.float32
 
     x = pl.pallas_call(
         functools.partial(pack_body, width=width, lanes=lanes, owners=owners),
+        in_specs=[pl.BlockSpec(memory_space=pltpu.HBM)] * 3,
         out_shape=pltpu.VMEM((q_dev, width + lanes), jnp.bfloat16),
+        scratch_shapes=[
+            pltpu.VMEM(cand_owner.shape, jnp.int32),
+            pltpu.VMEM(cand_row.shape, jnp.int32),
+            pltpu.SemaphoreType.DMA((3,)),
+        ],
         compiler_params=SMALL,
         name="pack",
-    )(queries, cand_owner, cand_row)
+    )(*in_hbm(queries, cand_owner, cand_row))
+    r_dev = slab.shape[0]
+    chunk = 512
+    cuts = [0, 3 * r_dev // 8, 7 * r_dev // 8, r_dev]
+    pieces = []
     for offs in stages[:-1]:
-        x = join([x] + [swap(x, off, devices) for off in offs])
+        got = [swap(x, off, devices) for off in offs]
+        if len(pieces) < 2:
+            at = len(pieces)
+            pieces.append(load(slab, cuts[at], cuts[at + 1] - cuts[at]))
+        x = join([x] + got)
     y = swap(x, stages[-1][0], devices)
+    pieces.append(load(slab, cuts[2], cuts[3] - cuts[2]))
 
     n_half = x.shape[0]
     half = min(n_half, 128)
     wide = PREFIX + tail
-    r_dev = slab.shape[0]
-    chunk = 512
     pair = [pl.BlockSpec((half, width + lanes), lambda i: (i, 0))] * 2
     if n_half == half:
         pair = [pl.BlockSpec(memory_space=pltpu.VMEM)] * 2
@@ -210,18 +249,16 @@
     keep, send = pl.pallas_call(
         functools.partial(score_body, width=width, owners=owners, chunk=chunk),
         grid=(n_half // half,),
-        in_specs=[pl.BlockSpec(memory_space=pltpu.SMEM), *pair, pl.BlockSpec(memory_space=pl.ANY)],
+        in_specs=[*pair, *[pl.BlockSpec(memory_space=pltpu.VMEM)] * 3],
         out_specs=outs,
         out_shape=(shape, shape),
         scratch_shapes=[
             pltpu.VMEM((2 * half, width + lanes), jnp.bfloat16),
-            pltpu.VMEM((r_dev, width), jnp.bfloat16),
             pltpu.VMEM((2 * half, r_dev), f32),
-            pltpu.SemaphoreType.DMA((r_dev // chunk,)),
         ],
-        compiler_params=pltpu.CompilerParams(vmem_limit_bytes=36000 * 1024),
+        compiler_params=pltpu.CompilerParams(vmem_limit_bytes=20 << 20),
         name="score",
-    )(me, x, y, slab)
+    )(x, y, *in_vmem(*pieces))
 
     parts = [keep, swap(send, stages[-1][0], devices)]
     for offs in reversed(stages[:-1]):

time: 56.8 us -> 53.1 us (0.935)
  local copies, waits for them, and re-layouts: 7.9 us -> 0.01 us
  Pallas kernels: 11.1 us -> 17 us
  waiting for transfers between devices: 19.2 us -> 17 us
    unnamed x10 -> x2, local copies, waits for them, and re-layouts: 7.9 us -> 0.01 us
    pallas_call x0 -> x3, Pallas kernels: none -> 7.79 us  [load(): pl.pallas_call(functools.partial(load_body, first=first), in_specs=[pl.Bl...]
    pallas_call x1, Pallas kernels: 9.72 us -> 7.16 us  [on_device(): pl.pallas_call(functools.partial(score_body, width=width, owners=owners,...]
    ppermute x14, waiting for transfers between devices: 19.2 us -> 17 us  [swap(): return lax.ppermute(x, AXES, [(d, d ^ off) for d in range(devices)])]
    pallas_call x1, Pallas kernels: 0.25 us -> 0.99 us  [on_device(): pl.pallas_call(functools.partial(pack_body, width=width, lanes=lanes, own...]
  transfers between devices with their start and end apart: 14 -> 14, of which waited for: 11 -> 10; matrix products, arithmetic and copies ran while one was open for 0% -> 0% of each run, Pallas kernels for 0% -> 15%
where the time goes in v1:
time: 53.1 us; the launch traced here: 52.8 us
  starting transfers between devices  18 us (34%)
  Pallas kernels  17 us (32%)
  waiting for transfers between devices  17 us (32%)
  between operations  0.73 us (1%)
    ppermute x14, starting transfers between devices, swap(): return lax.ppermute(x, AXES, [(d, d ^ off) for d in range(devices)])  18 us
    ppermute x14, waiting for transfers between devices, swap(): return lax.ppermute(x, AXES, [(d, d ^ off) for d in range(devices)])  17 us
    pallas_call x3, Pallas kernels, load(): pl.pallas_call(functools.partial(load_body, first=first), in_specs=[pl.Bl...  7.79 us
    pallas_call x1, Pallas kernels, on_device(): pl.pallas_call(functools.partial(score_body, width=width, owners=owners,...  7.16 us
  transfers between devices with their start and end apart: 14, of which 10 were waited for; matrix products, arithmetic and copies ran while one was open for 0% of the time, Pallas kernels for 15%

profile of v1, /device:TPU:0, one launch (start us, length us, event | category | flops | bytes accessed | tf_op | source)
XLA Modules:
  0.0 52.8 jit_solution(6435066326895748812)
XLA Ops:
  0.6 1.0 %pack.1.refs_0_ = bf16[8,2176]{1,0:T(8,128)(2,1)S(1)} custom-call(bf16[8,2048]{1,0:T(8,128)(2,1)} %q_hbm.1, s32[8,32]{1,0:T(8,128)} %owner_ref.1, s32[8,32]{1,0:T(8,128)} %row_hbm.1), custom_call_target="tpu_custom_call" | custom-call | tf_op jit(solution)/shard_map/pack/pallas_call | solution.py:212
  1.6 5.1 %collective-permute-start.2 = (bf16[8,2176]{1,0:T(8,128)(2,1)S(1)}, bf16[8,2176]{1,0:T(8,128)(2,1)S(1)}, u32[]{:S(2)}, u32[]{:S(2)}) collective-permute-start(bf16[8,2176]{1,0:T(8,128)(2,1)S(1)} %pack.1.refs_0_), channel_id=1, source_target_pairs={{0,3},{1,2},{2,1},{3,0},{4,7},{5,6},{6,5},{7,4},{8,11},{9,10},{10,... | collective-permute-start | bytes 104456 | tf_op jit(solution)/shard_map/ppermute | solution.py:31
  6.8 0.6 %collective-permute-start = (bf16[8,2176]{1,0:T(8,128)(2,1)S(1)}, bf16[8,2176]{1,0:T(8,128)(2,1)S(1)}, u32[]{:S(2)}, u32[]{:S(2)}) collective-permute-start(bf16[8,2176]{1,0:T(8,128)(2,1)S(1)} %pack.1.refs_0_), channel_id=1, source_target_pairs={{0,1},{1,0},{2,3},{3,2},{4,5},{5,4},{6,7},{7,6},{8,9},{9,8},{10,11... | collective-permute-start | bytes 104456 | tf_op jit(solution)/shard_map/ppermute | solution.py:31
  7.4 1.3 %collective-permute-done.2.refs_3_ = bf16[8,2176]{1,0:T(8,128)(2,1)S(1)} collective-permute-done((bf16[8,2176]{1,0:T(8,128)(2,1)S(1)}, bf16[8,2176]{1,0:T(8,128)(2,1)S(1)}, u32[]{:S(2)}, u32[]{:S(2)}) %collective-permute-start.2) | collective-permute-done | bytes 34848 | tf_op jit(solution)/shard_map/ppermute | solution.py:31
  8.7 2.9 %collective-permute-done.1.refs_2_ = bf16[8,2176]{1,0:T(8,128)(2,1)S(1)} collective-permute-done((bf16[8,2176]{1,0:T(8,128)(2,1)S(1)}, bf16[8,2176]{1,0:T(8,128)(2,1)S(1)}, u32[]{:S(2)}, u32[]{:S(2)}) %collective-permute-start.1) | collective-permute-done | bytes 34848 | tf_op jit(solution)/shard_map/ppermute | solution.py:31
  11.6 2.5 %collective-permute-start.5 = (bf16[32,2176]{1,0:T(8,128)(2,1)S(1)}, bf16[32,2176]{1,0:T(8,128)(2,1)S(1)}, u32[]{:S(2)}, u32[]{:S(2)}) collective-permute-start(bf16[32,2176]{1,0:T(8,128)(2,1)S(1)} %join.2.refs_0_), channel_id=1, source_target_pairs={{0,24},{1,25},{2,26},{3,27},{4,28},{5,29},{6,30},{7,31},{8,16},{9,... | collective-permute-start | bytes 417800 | tf_op jit(solution)/shard_map/ppermute | solution.py:31
  14.1 0.5 collective-permute-start.4
  14.6 0.5 %collective-permute-start.3 = (bf16[32,2176]{1,0:T(8,128)(2,1)S(1)}, bf16[32,2176]{1,0:T(8,128)(2,1)S(1)}, u32[]{:S(2)}, u32[]{:S(2)}) collective-permute-start(bf16[32,2176]{1,0:T(8,128)(2,1)S(1)} %join.2.refs_0_), channel_id=1, source_target_pairs={{0,8},{1,9},{2,10},{3,11},{4,12},{5,13},{6,14},{7,15},{8,0},{9,1},... | collective-permute-start | bytes 417800 | tf_op jit(solution)/shard_map/ppermute | solution.py:31
  15.2 3.9 %collective-permute-done.5.refs_3_ = bf16[32,2176]{1,0:T(8,128)(2,1)S(1)} collective-permute-done((bf16[32,2176]{1,0:T(8,128)(2,1)S(1)}, bf16[32,2176]{1,0:T(8,128)(2,1)S(1)}, u32[]{:S(2)}, u32[]{:S(2)}) %collective-permute-start.5) | collective-permute-done | bytes 139296 | tf_op jit(solution)/shard_map/ppermute | solution.py:31
  19.1 0.8 %collective-permute-done.4.refs_2_ = bf16[32,2176]{1,0:T(8,128)(2,1)S(1)} collective-permute-done((bf16[32,2176]{1,0:T(8,128)(2,1)S(1)}, bf16[32,2176]{1,0:T(8,128)(2,1)S(1)}, u32[]{:S(2)}, u32[]{:S(2)}) %collective-permute-start.4) | collective-permute-done | bytes 139296 | tf_op jit(solution)/shard_map/ppermute | solution.py:31
  20.0 0.1 collective-permute-start.6
  20.0 1.6 %load.5.rows_c = bf16[512,2048]{1,0:T(8,128)(2,1)S(1)} custom-call(bf16[4096,2048]{1,0:T(8,128)(2,1)} %from_ref.5), custom_call_target="tpu_custom_call" | custom-call | bytes 2097152 | tf_op jit(solution)/shard_map/load/pallas_call | solution.py:68
  21.6 2.8 %load.3.rows_a = bf16[1536,2048]{1,0:T(8,128)(2,1)S(1)} custom-call(bf16[4096,2048]{1,0:T(8,128)(2,1)} %from_ref.5), custom_call_target="tpu_custom_call" | custom-call | bytes 6291456 | tf_op jit(solution)/shard_map/load/pallas_call | solution.py:68
  24.4 3.4 %load.4.rows_b = bf16[2048,2048]{1,0:T(8,128)(2,1)S(1)} custom-call(bf16[4096,2048]{1,0:T(8,128)(2,1)} %from_ref.5), custom_call_target="tpu_custom_call" | custom-call | bytes 8388608 | tf_op jit(solution)/shard_map/load/pallas_call | solution.py:68
  27.9 0.0 copy-start
  27.9 7.2 %score.1 = (f32[128,384]{1,0:T(8,128)S(1)}, f32[128,384]{1,0:T(8,128)S(1)}) custom-call(bf16[128,2176]{1,0:T(8,128)(2,1)S(1)} %join.3.x_ref, bf16[128,2176]{1,0:T(8,128)(2,1)S(1)} %collective-permute-done.6.y_ref, bf16[1536,2048]{1,0:T(8,128)(2,1)S(1)} %load.3.rows_a, bf16[2048,2048]{1,0:T(8,128)(2,1)S(1)} %load.4.rows_b, bf16[512,2048]{1,0:T(8,128)(2,1)S(1)} %load.5.rows_c), custom_call_target="tpu_custom_call" | custom-call | tf_op jit(solution)/shard_map/score/pallas_call | solution.py:249
  35.0 0.6 %collective-permute-start.7 = (f32[128,384]{1,0:T(8,128)S(1)}, f32[128,384]{1,0:T(8,128)S(1)}, u32[]{:S(2)}, u32[]{:S(2)}) collective-permute-start(f32[128,384]{1,0:T(8,128)S(1)} %get-tuple-element.17), channel_id=1, source_target_pairs={{0,4},{1,5},{2,6},{3,7},{4,0},{5,1},{6,2},{7,3},{8,12},{9,13},{10,... | collective-permute-start | bytes 589832 | tf_op jit(solution)/shard_map/ppermute | solution.py:31
  35.6 1.1 %collective-permute-done.7.refs_1_ = f32[128,384]{1,0:T(8,128)S(1)} collective-permute-done((f32[128,384]{1,0:T(8,128)S(1)}, f32[128,384]{1,0:T(8,128)S(1)}, u32[]{:S(2)}, u32[]{:S(2)}) %collective-permute-start.7) | collective-permute-done | bytes 196640 | tf_op jit(solution)/shard_map/ppermute | solution.py:31
  36.7 0.1 merge.2
  36.8 1.3 %collective-permute-start.8 = (f32[32,384]{1,0:T(8,128)S(1)}, f32[32,384]{1,0:T(8,128)S(1)}, u32[]{:S(2)}, u32[]{:S(2)}) collective-permute-start(f32[32,384]{1,0:T(8,128)S(1)} %get-tuple-element.19), channel_id=1, source_target_pairs={{0,8},{1,9},{2,10},{3,11},{4,12},{5,13},{6,14},{7,15},{8,0},{9,1},... | collective-permute-start | bytes 147464 | tf_op jit(solution)/shard_map/ppermute | solution.py:31
  38.2 0.7 %collective-permute-start.9 = (f32[32,384]{1,0:T(8,128)S(1)}, f32[32,384]{1,0:T(8,128)S(1)}, u32[]{:S(2)}, u32[]{:S(2)}) collective-permute-start(f32[32,384]{1,0:T(8,128)S(1)} %get-tuple-element.20), channel_id=1, source_target_pairs={{0,16},{1,17},{2,18},{3,19},{4,20},{5,21},{6,22},{7,23},{8,24},{9,... | collective-permute-start | bytes 147464 | tf_op jit(solution)/shard_map/ppermute | solution.py:31
  38.8 1.5 %collective-permute-start.10 = (f32[32,384]{1,0:T(8,128)S(1)}, f32[32,384]{1,0:T(8,128)S(1)}, u32[]{:S(2)}, u32[]{:S(2)}) collective-permute-start(f32[32,384]{1,0:T(8,128)S(1)} %get-tuple-element.21), channel_id=1, source_target_pairs={{0,24},{1,25},{2,26},{3,27},{4,28},{5,29},{6,30},{7,31},{8,16},{9,... | collective-permute-start | bytes 147464 | tf_op jit(solution)/shard_map/ppermute | solution.py:31
  40.4 0.6 %collective-permute-done.8.refs_1_ = f32[32,384]{1,0:T(8,128)S(1)} collective-permute-done((f32[32,384]{1,0:T(8,128)S(1)}, f32[32,384]{1,0:T(8,128)S(1)}, u32[]{:S(2)}, u32[]{:S(2)}) %collective-permute-start.8) | collective-permute-done | bytes 49184 | tf_op jit(solution)/shard_map/ppermute | solution.py:31
  41.0 1.8 %collective-permute-done.9.refs_2_ = f32[32,384]{1,0:T(8,128)S(1)} collective-permute-done((f32[32,384]{1,0:T(8,128)S(1)}, f32[32,384]{1,0:T(8,128)S(1)}, u32[]{:S(2)}, u32[]{:S(2)}) %collective-permute-start.9) | collective-permute-done | bytes 49184 | tf_op jit(solution)/shard_map/ppermute | solution.py:31
  42.8 1.0 %collective-permute-done.10.refs_3_ = f32[32,384]{1,0:T(8,128)S(1)} collective-permute-done((f32[32,384]{1,0:T(8,128)S(1)}, f32[32,384]{1,0:T(8,128)S(1)}, u32[]{:S(2)}, u32[]{:S(2)}) %collective-permute-start.10) | collective-permute-done | bytes 49184 | tf_op jit(solution)/shard_map/ppermute | solution.py:31
  43.8 0.1 merge.3
  43.9 0.2 collective-permute-start.11
  44.1 2.3 %collective-permute-start.12 = (f32[8,384]{1,0:T(8,128)S(1)}, f32[8,384]{1,0:T(8,128)S(1)}, u32[]{:S(2)}, u32[]{:S(2)}) collective-permute-start(f32[8,384]{1,0:T(8,128)S(1)} %get-tuple-element.24), channel_id=1, source_target_pairs={{0,2},{1,3},{2,0},{3,1},{4,6},{5,7},{6,4},{7,5},{8,10},{9,11},{10,... | collective-permute-start | bytes 36872 | tf_op jit(solution)/shard_map/ppermute | solution.py:31
  46.4 1.9 %collective-permute-start.13 = (f32[8,384]{1,0:T(8,128)S(1)}, f32[8,384]{1,0:T(8,128)S(1)}, u32[]{:S(2)}, u32[]{:S(2)}) collective-permute-start(f32[8,384]{1,0:T(8,128)S(1)} %get-tuple-element.25), channel_id=1, source_target_pairs={{0,3},{1,2},{2,1},{3,0},{4,7},{5,6},{6,5},{7,4},{8,11},{9,10},{10,... | collective-permute-start | bytes 36872 | tf_op jit(solution)/shard_map/ppermute | solution.py:31
  48.4 0.3 collective-permute-done.12.refs_2_
  48.7 3.2 %collective-permute-done.13.refs_3_ = f32[8,384]{1,0:T(8,128)S(1)} collective-permute-done((f32[8,384]{1,0:T(8,128)S(1)}, f32[8,384]{1,0:T(8,128)S(1)}, u32[]{:S(2)}, u32[]{:S(2)}) %collective-permute-start.13) | collective-permute-done | bytes 12320 | tf_op jit(solution)/shard_map/ppermute | solution.py:31
  51.9 0.8 %finish.1 = (f32[8,256]{1,0:T(8,128)}, f32[1,8]{1,0:T(1,128)}, f32[8,32]{1,0:T(8,128)}) custom-call(s32[8,32]{1,0:T(8,128)S(1)} %copy-done, f32[8,384]{1,0:T(8,128)S(1)} %get-tuple-element.22.refs_0_, f32[8,384]{1,0:T(8,128)S(1)} %collective-permute-done.11.refs_1_, f32[8,384]{1,0:T(8,128)S(1)} %collective-permute-done.12.refs_2_, ...), custom_call_target="tpu_custom_call" | custom-call | tf_op jit(solution)/shard_map/finish/pallas_call | solution.py:273
  (8 shorter events, 0.1 us)
Async XLA Ops:
  1.6 7.1 %collective-permute-start.2 = (bf16[8,2176]{1,0:T(8,128)(2,1)S(1)}, bf16[8,2176]{1,0:T(8,128)(2,1)S(1)}, u32[]{:S(2)}, u32[]{:S(2)}) collective-permute-start(bf16[8,2176]{1,0:T(8,128)(2,1)S(1)} %pack.1.refs_0_), channel_id=1, source_target_pairs={{0,3},{1,2},{2,1},{3,0},{4,7},{5,6},{6,5},{7,4},{8,11},{9,10},{10,... | collective-permute-start | bytes 104456 | tf_op jit(solution)/shard_map/ppermute | solution.py:31
  6.8 4.8 %collective-permute-start.1 = (bf16[8,2176]{1,0:T(8,128)(2,1)S(1)}, bf16[8,2176]{1,0:T(8,128)(2,1)S(1)}, u32[]{:S(2)}, u32[]{:S(2)}) collective-permute-start(bf16[8,2176]{1,0:T(8,128)(2,1)S(1)} %pack.1.refs_0_), channel_id=1, source_target_pairs={{0,2},{1,3},{2,0},{3,1},{4,6},{5,7},{6,4},{7,5},{8,10},{9,11},{10,... | collective-permute-start | bytes 104456 | tf_op jit(solution)/shard_map/ppermute | solution.py:31
  6.8 4.8 %collective-permute-start = (bf16[8,2176]{1,0:T(8,128)(2,1)S(1)}, bf16[8,2176]{1,0:T(8,128)(2,1)S(1)}, u32[]{:S(2)}, u32[]{:S(2)}) collective-permute-start(bf16[8,2176]{1,0:T(8,128)(2,1)S(1)} %pack.1.refs_0_), channel_id=1, source_target_pairs={{0,1},{1,0},{2,3},{3,2},{4,5},{5,4},{6,7},{7,6},{8,9},{9,8},{10,11... | collective-permute-start | bytes 104456 | tf_op jit(solution)/shard_map/ppermute | solution.py:31
  11.6 7.5 %collective-permute-start.5 = (bf16[32,2176]{1,0:T(8,128)(2,1)S(1)}, bf16[32,2176]{1,0:T(8,128)(2,1)S(1)}, u32[]{:S(2)}, u32[]{:S(2)}) collective-permute-start(bf16[32,2176]{1,0:T(8,128)(2,1)S(1)} %join.2.refs_0_), channel_id=1, source_target_pairs={{0,24},{1,25},{2,26},{3,27},{4,28},{5,29},{6,30},{7,31},{8,16},{9,... | collective-permute-start | bytes 417800 | tf_op jit(solution)/shard_map/ppermute | solution.py:31
  14.1 5.8 %collective-permute-start.4 = (bf16[32,2176]{1,0:T(8,128)(2,1)S(1)}, bf16[32,2176]{1,0:T(8,128)(2,1)S(1)}, u32[]{:S(2)}, u32[]{:S(2)}) collective-permute-start(bf16[32,2176]{1,0:T(8,128)(2,1)S(1)} %join.2.refs_0_), channel_id=1, source_target_pairs={{0,16},{1,17},{2,18},{3,19},{4,20},{5,21},{6,22},{7,23},{8,24},{9,... | collective-permute-start | bytes 417800 | tf_op jit(solution)/shard_map/ppermute | solution.py:31
  14.6 5.3 %collective-permute-start.3 = (bf16[32,2176]{1,0:T(8,128)(2,1)S(1)}, bf16[32,2176]{1,0:T(8,128)(2,1)S(1)}, u32[]{:S(2)}, u32[]{:S(2)}) collective-permute-start(bf16[32,2176]{1,0:T(8,128)(2,1)S(1)} %join.2.refs_0_), channel_id=1, source_target_pairs={{0,8},{1,9},{2,10},{3,11},{4,12},{5,13},{6,14},{7,15},{8,0},{9,1},... | collective-permute-start | bytes 417800 | tf_op jit(solution)/shard_map/ppermute | solution.py:31
  20.0 7.9 %collective-permute-start.6 = (bf16[128,2176]{1,0:T(8,128)(2,1)S(1)}, bf16[128,2176]{1,0:T(8,128)(2,1)S(1)}, u32[]{:S(2)}, u32[]{:S(2)}) collective-permute-start(bf16[128,2176]{1,0:T(8,128)(2,1)S(1)} %join.3.x_ref), channel_id=1, source_target_pairs={{0,4},{1,5},{2,6},{3,7},{4,0},{5,1},{6,2},{7,3},{8,12},{9,13},{10,... | collective-permute-start | bytes 1671176 | tf_op jit(solution)/shard_map/ppermute | solution.py:31
  27.9 24.1 %copy-start = (s32[8,32]{1,0:T(8,128)S(1)}, s32[8,32]{1,0:T(8,128)}, u32[]{:S(2)}) copy-start(s32[8,32]{1,0:T(8,128)} %owner_ref.1) | copy-start | bytes 3076
  35.0 1.6 %collective-permute-start.7 = (f32[128,384]{1,0:T(8,128)S(1)}, f32[128,384]{1,0:T(8,128)S(1)}, u32[]{:S(2)}, u32[]{:S(2)}) collective-permute-start(f32[128,384]{1,0:T(8,128)S(1)} %get-tuple-element.17), channel_id=1, source_target_pairs={{0,4},{1,5},{2,6},{3,7},{4,0},{5,1},{6,2},{7,3},{8,12},{9,13},{10,... | collective-permute-start | bytes 589832 | tf_op jit(solution)/shard_map/ppermute | solution.py:31
  36.8 4.2 %collective-permute-start.8 = (f32[32,384]{1,0:T(8,128)S(1)}, f32[32,384]{1,0:T(8,128)S(1)}, u32[]{:S(2)}, u32[]{:S(2)}) collective-permute-start(f32[32,384]{1,0:T(8,128)S(1)} %get-tuple-element.19), channel_id=1, source_target_pairs={{0,8},{1,9},{2,10},{3,11},{4,12},{5,13},{6,14},{7,15},{8,0},{9,1},... | collective-permute-start | bytes 147464 | tf_op jit(solution)/shard_map/ppermute | solution.py:31
  38.2 4.6 %collective-permute-start.9 = (f32[32,384]{1,0:T(8,128)S(1)}, f32[32,384]{1,0:T(8,128)S(1)}, u32[]{:S(2)}, u32[]{:S(2)}) collective-permute-start(f32[32,384]{1,0:T(8,128)S(1)} %get-tuple-element.20), channel_id=1, source_target_pairs={{0,16},{1,17},{2,18},{3,19},{4,20},{5,21},{6,22},{7,23},{8,24},{9,... | collective-permute-start | bytes 147464 | tf_op jit(solution)/shard_map/ppermute | solution.py:31
  38.8 5.0 %collective-permute-start.10 = (f32[32,384]{1,0:T(8,128)S(1)}, f32[32,384]{1,0:T(8,128)S(1)}, u32[]{:S(2)}, u32[]{:S(2)}) collective-permute-start(f32[32,384]{1,0:T(8,128)S(1)} %get-tuple-element.21), channel_id=1, source_target_pairs={{0,24},{1,25},{2,26},{3,27},{4,28},{5,29},{6,30},{7,31},{8,16},{9,... | collective-permute-start | bytes 147464 | tf_op jit(solution)/shard_map/ppermute | solution.py:31
  43.9 4.5 %collective-permute-start.11 = (f32[8,384]{1,0:T(8,128)S(1)}, f32[8,384]{1,0:T(8,128)S(1)}, u32[]{:S(2)}, u32[]{:S(2)}) collective-permute-start(f32[8,384]{1,0:T(8,128)S(1)} %get-tuple-element.23), channel_id=1, source_target_pairs={{0,1},{1,0},{2,3},{3,2},{4,5},{5,4},{6,7},{7,6},{8,9},{9,8},{10,11... | collective-permute-start | bytes 36872 | tf_op jit(solution)/shard_map/ppermute | solution.py:31
  44.1 4.6 %collective-permute-start.12 = (f32[8,384]{1,0:T(8,128)S(1)}, f32[8,384]{1,0:T(8,128)S(1)}, u32[]{:S(2)}, u32[]{:S(2)}) collective-permute-start(f32[8,384]{1,0:T(8,128)S(1)} %get-tuple-element.24), channel_id=1, source_target_pairs={{0,2},{1,3},{2,0},{3,1},{4,6},{5,7},{6,4},{7,5},{8,10},{9,11},{10,... | collective-permute-start | bytes 36872 | tf_op jit(solution)/shard_map/ppermute | solution.py:31
  46.4 5.5 %collective-permute-start.13 = (f32[8,384]{1,0:T(8,128)S(1)}, f32[8,384]{1,0:T(8,128)S(1)}, u32[]{:S(2)}, u32[]{:S(2)}) collective-permute-start(f32[8,384]{1,0:T(8,128)S(1)} %get-tuple-element.25), channel_id=1, source_target_pairs={{0,3},{1,2},{2,1},{3,0},{4,7},{5,6},{6,5},{7,4},{8,11},{9,10},{10,... | collective-permute-start | bytes 36872 | tf_op jit(solution)/shard_map/ppermute | solution.py:31

commit v2 on v1

--- a/solution.py
+++ b/solution.py
@@ -32,6 +32,13 @@
 
 
 SMALL = pltpu.CompilerParams(vmem_limit_bytes=16 << 20)
+
+
+def swaps(arrays, offs, devices):
+    out = []
+    for x, off in zip(arrays, offs):
+        out.append(swap(x, off, devices))
+    return out
 
 
 def in_vmem(*arrays):
@@ -128,22 +135,22 @@
             g_ref[:, :PREFIX], ref[own, :PREFIX], contract, preferred_element_type=jnp.float32
         )
         logit_ref[:, at] = logits
+        for s in range(chunk // 128):
+            best = jnp.maximum(best, logits[:, s * 128 : (s + 1) * 128])
+    top = jnp.max(best, axis=1, keepdims=True)
+    acc = jnp.zeros((n_q, PREFIX), jnp.float32)
+    total = jnp.zeros((n_q, 128), jnp.float32)
+    col = lax.broadcasted_iota(jnp.int32, (n_q, 128), 1)
+    for c in range(n_chunks):
+        at = slice(c * chunk, (c + 1) * chunk)
+        ref, own = rows[c]
         full = lax.dot_general(
             g_ref[:, PREFIX:width], ref[own, PREFIX:], contract, preferred_element_type=jnp.float32
         )
-        full = full + logits
-        col = lax.broadcasted_iota(jnp.int32, (n_q, 128), 1)
+        full = full + logit_ref[:, at]
         for s in range(chunk // 128):
-            part = slice(s * 128, (s + 1) * 128)
-            best = jnp.maximum(best, logits[:, part])
-            score += jnp.where(col + (c * chunk + s * 128) == want, full[:, part], 0.0)
-    top = jnp.max(best, axis=1, keepdims=True)
-    score = jnp.sum(score, axis=1, keepdims=True) * width ** (-0.5)
-    acc = jnp.zeros((n_q, PREFIX), jnp.float32)
-    total = jnp.zeros((n_q, 128), jnp.float32)
-    for c in range(n_chunks):
-        at = slice(c * chunk, (c + 1) * chunk)
-        ref, own = rows[c]
+            part = full[:, s * 128 : (s + 1) * 128]
+            score += jnp.where(col + (c * chunk + s * 128) == want, part, 0.0)
         weights = jnp.exp((logit_ref[:, at] - top) * scale)
         for s in range(chunk // 128):
             total += weights[:, s * 128 : (s + 1) * 128]
@@ -151,6 +158,7 @@
             weights.astype(jnp.bfloat16), ref[own, :PREFIX], preferred_element_type=jnp.float32
         )
     total = jnp.sum(total, axis=1, keepdims=True)
+    score = jnp.sum(score, axis=1, keepdims=True) * width ** (-0.5)
     tail = keep_ref.shape[1] - PREFIX
     lane = lax.broadcasted_iota(jnp.int32, (n_q, tail), 1)
     rest = jnp.where(
@@ -222,11 +230,11 @@
         name="pack",
     )(*in_hbm(queries, cand_owner, cand_row))
     r_dev = slab.shape[0]
-    chunk = 512
-    cuts = [0, 3 * r_dev // 8, 7 * r_dev // 8, r_dev]
+    chunk = r_dev // 16
+    cuts = [0, 4 * chunk, 14 * chunk, r_dev]
     pieces = []
     for offs in stages[:-1]:
-        got = [swap(x, off, devices) for off in offs]
+        got = swaps([x] * len(offs), offs, devices)
         if len(pieces) < 2:
             at = len(pieces)
             pieces.append(load(slab, cuts[at], cuts[at + 1] - cuts[at]))
@@ -269,7 +277,7 @@
             compiler_params=SMALL,
             name="merge",
         )(*in_vmem(*parts))
-        parts = [keep] + [swap(s, off, devices) for s, off in zip(sends, offs)]
+        parts = [keep] + swaps(sends, offs, devices)
     pooled, lse, margin = pl.pallas_call(
         functools.partial(finish_body, owners=owners),
         out_shape=(

time: 53.1 us -> 51.6 us (0.972)
  Pallas kernels: 17 us -> 15.6 us
    pallas_call x1, Pallas kernels: 7.16 us -> 5.74 us  [on_device(): pl.pallas_call(functools.partial(score_body, width=width, owners=owners,...]
where the time goes in v2:
time: 51.6 us; the launch traced here: 51.3 us
  starting transfers between devices  18 us (35%)
  waiting for transfers between devices  17 us (33%)
  Pallas kernels  15.6 us (30%)
  between operations  0.73 us (1%)
    ppermute x14, starting transfers between devices, swap(): return lax.ppermute(x, AXES, [(d, d ^ off) for d in range(devices)])  18 us
    ppermute x14, waiting for transfers between devices, swap(): return lax.ppermute(x, AXES, [(d, d ^ off) for d in range(devices)])  17 us
    pallas_call x3, Pallas kernels, load(): pl.pallas_call(functools.partial(load_body, first=first), in_specs=[pl.Bl...  7.79 us
    pallas_call x1, Pallas kernels, on_device(): pl.pallas_call(functools.partial(score_body, width=width, owners=owners,...  5.74 us
  transfers between devices with their start and end apart: 14, of which 10 were waited for; matrix products, arithmetic and copies ran while one was open for 0% of the time, Pallas kernels for 15%

profile of v2, /device:TPU:0, one launch (start us, length us, event | category | flops | bytes accessed | tf_op | source)
XLA Modules:
  0.0 51.3 jit_solution(12218497298171492958)
XLA Ops:
  0.6 1.0 %pack.1.refs_0_ = bf16[8,2176]{1,0:T(8,128)(2,1)S(1)} custom-call(bf16[8,2048]{1,0:T(8,128)(2,1)} %q_hbm.1, s32[8,32]{1,0:T(8,128)} %owner_ref.1, s32[8,32]{1,0:T(8,128)} %row_hbm.1), custom_call_target="tpu_custom_call" | custom-call | tf_op jit(solution)/shard_map/pack/pallas_call | solution.py:220
  1.6 5.1 %collective-permute-start.2 = (bf16[8,2176]{1,0:T(8,128)(2,1)S(1)}, bf16[8,2176]{1,0:T(8,128)(2,1)S(1)}, u32[]{:S(2)}, u32[]{:S(2)}) collective-permute-start(bf16[8,2176]{1,0:T(8,128)(2,1)S(1)} %pack.1.refs_0_), channel_id=1, source_target_pairs={{0,3},{1,2},{2,1},{3,0},{4,7},{5,6},{6,5},{7,4},{8,11},{9,10},{10,... | collective-permute-start | bytes 104456 | tf_op jit(solution)/shard_map/ppermute | solution.py:31
  6.8 0.6 %collective-permute-start = (bf16[8,2176]{1,0:T(8,128)(2,1)S(1)}, bf16[8,2176]{1,0:T(8,128)(2,1)S(1)}, u32[]{:S(2)}, u32[]{:S(2)}) collective-permute-start(bf16[8,2176]{1,0:T(8,128)(2,1)S(1)} %pack.1.refs_0_), channel_id=1, source_target_pairs={{0,1},{1,0},{2,3},{3,2},{4,5},{5,4},{6,7},{7,6},{8,9},{9,8},{10,11... | collective-permute-start | bytes 104456 | tf_op jit(solution)/shard_map/ppermute | solution.py:31
  7.4 1.3 %collective-permute-done.2.refs_3_ = bf16[8,2176]{1,0:T(8,128)(2,1)S(1)} collective-permute-done((bf16[8,2176]{1,0:T(8,128)(2,1)S(1)}, bf16[8,2176]{1,0:T(8,128)(2,1)S(1)}, u32[]{:S(2)}, u32[]{:S(2)}) %collective-permute-start.2) | collective-permute-done | bytes 34848 | tf_op jit(solution)/shard_map/ppermute | solution.py:31
  8.7 2.9 %collective-permute-done.1.refs_2_ = bf16[8,2176]{1,0:T(8,128)(2,1)S(1)} collective-permute-done((bf16[8,2176]{1,0:T(8,128)(2,1)S(1)}, bf16[8,2176]{1,0:T(8,128)(2,1)S(1)}, u32[]{:S(2)}, u32[]{:S(2)}) %collective-permute-start.1) | collective-permute-done | bytes 34848 | tf_op jit(solution)/shard_map/ppermute | solution.py:31
  11.6 2.5 %collective-permute-start.5 = (bf16[32,2176]{1,0:T(8,128)(2,1)S(1)}, bf16[32,2176]{1,0:T(8,128)(2,1)S(1)}, u32[]{:S(2)}, u32[]{:S(2)}) collective-permute-start(bf16[32,2176]{1,0:T(8,128)(2,1)S(1)} %join.2.refs_0_), channel_id=1, source_target_pairs={{0,24},{1,25},{2,26},{3,27},{4,28},{5,29},{6,30},{7,31},{8,16},{9,... | collective-permute-start | bytes 417800 | tf_op jit(solution)/shard_map/ppermute | solution.py:31
  14.1 0.5 collective-permute-start.4
  14.6 0.5 %collective-permute-start.3 = (bf16[32,2176]{1,0:T(8,128)(2,1)S(1)}, bf16[32,2176]{1,0:T(8,128)(2,1)S(1)}, u32[]{:S(2)}, u32[]{:S(2)}) collective-permute-start(bf16[32,2176]{1,0:T(8,128)(2,1)S(1)} %join.2.refs_0_), channel_id=1, source_target_pairs={{0,8},{1,9},{2,10},{3,11},{4,12},{5,13},{6,14},{7,15},{8,0},{9,1},... | collective-permute-start | bytes 417800 | tf_op jit(solution)/shard_map/ppermute | solution.py:31
  15.2 3.9 %collective-permute-done.5.refs_3_ = bf16[32,2176]{1,0:T(8,128)(2,1)S(1)} collective-permute-done((bf16[32,2176]{1,0:T(8,128)(2,1)S(1)}, bf16[32,2176]{1,0:T(8,128)(2,1)S(1)}, u32[]{:S(2)}, u32[]{:S(2)}) %collective-permute-start.5) | collective-permute-done | bytes 139296 | tf_op jit(solution)/shard_map/ppermute | solution.py:31
  19.1 0.8 %collective-permute-done.4.refs_2_ = bf16[32,2176]{1,0:T(8,128)(2,1)S(1)} collective-permute-done((bf16[32,2176]{1,0:T(8,128)(2,1)S(1)}, bf16[32,2176]{1,0:T(8,128)(2,1)S(1)}, u32[]{:S(2)}, u32[]{:S(2)}) %collective-permute-start.4) | collective-permute-done | bytes 139296 | tf_op jit(solution)/shard_map/ppermute | solution.py:31
  20.0 0.1 collective-permute-start.6
  20.0 1.6 %load.5.rows_c = bf16[512,2048]{1,0:T(8,128)(2,1)S(1)} custom-call(bf16[4096,2048]{1,0:T(8,128)(2,1)} %from_ref.5), custom_call_target="tpu_custom_call" | custom-call | bytes 2097152 | tf_op jit(solution)/shard_map/load/pallas_call | solution.py:75
  21.6 2.2 %load.3.rows_a = bf16[1024,2048]{1,0:T(8,128)(2,1)S(1)} custom-call(bf16[4096,2048]{1,0:T(8,128)(2,1)} %from_ref.5), custom_call_target="tpu_custom_call" | custom-call | bytes 4194304 | tf_op jit(solution)/shard_map/load/pallas_call | solution.py:75
  23.9 4.0 %load.4.rows_b = bf16[2560,2048]{1,0:T(8,128)(2,1)S(1)} custom-call(bf16[4096,2048]{1,0:T(8,128)(2,1)} %from_ref.5), custom_call_target="tpu_custom_call" | custom-call | bytes 10485760 | tf_op jit(solution)/shard_map/load/pallas_call | solution.py:75
  27.9 0.0 copy-start
  27.9 5.7 %score.1 = (f32[128,384]{1,0:T(8,128)S(1)}, f32[128,384]{1,0:T(8,128)S(1)}) custom-call(bf16[128,2176]{1,0:T(8,128)(2,1)S(1)} %join.3.x_ref, bf16[128,2176]{1,0:T(8,128)(2,1)S(1)} %collective-permute-done.6.y_ref, bf16[1024,2048]{1,0:T(8,128)(2,1)S(1)} %load.3.rows_a, bf16[2560,2048]{1,0:T(8,128)(2,1)S(1)} %load.4.rows_b, bf16[512,2048]{1,0:T(8,128)(2,1)S(1)} %load.5.rows_c), custom_call_target="tpu_custom_call" | custom-call | tf_op jit(solution)/shard_map/score/pallas_call | solution.py:257
  33.6 0.6 %collective-permute-start.7 = (f32[128,384]{1,0:T(8,128)S(1)}, f32[128,384]{1,0:T(8,128)S(1)}, u32[]{:S(2)}, u32[]{:S(2)}) collective-permute-start(f32[128,384]{1,0:T(8,128)S(1)} %get-tuple-element.17), channel_id=1, source_target_pairs={{0,4},{1,5},{2,6},{3,7},{4,0},{5,1},{6,2},{7,3},{8,12},{9,13},{10,... | collective-permute-start | bytes 589832 | tf_op jit(solution)/shard_map/ppermute | solution.py:31
  34.2 1.1 %collective-permute-done.7.refs_1_ = f32[128,384]{1,0:T(8,128)S(1)} collective-permute-done((f32[128,384]{1,0:T(8,128)S(1)}, f32[128,384]{1,0:T(8,128)S(1)}, u32[]{:S(2)}, u32[]{:S(2)}) %collective-permute-start.7) | collective-permute-done | bytes 196640 | tf_op jit(solution)/shard_map/ppermute | solution.py:31
  35.3 0.1 merge.2
  35.4 1.3 %collective-permute-start.8 = (f32[32,384]{1,0:T(8,128)S(1)}, f32[32,384]{1,0:T(8,128)S(1)}, u32[]{:S(2)}, u32[]{:S(2)}) collective-permute-start(f32[32,384]{1,0:T(8,128)S(1)} %get-tuple-element.19), channel_id=1, source_target_pairs={{0,8},{1,9},{2,10},{3,11},{4,12},{5,13},{6,14},{7,15},{8,0},{9,1},... | collective-permute-start | bytes 147464 | tf_op jit(solution)/shard_map/ppermute | solution.py:31
  36.7 0.7 %collective-permute-start.9 = (f32[32,384]{1,0:T(8,128)S(1)}, f32[32,384]{1,0:T(8,128)S(1)}, u32[]{:S(2)}, u32[]{:S(2)}) collective-permute-start(f32[32,384]{1,0:T(8,128)S(1)} %get-tuple-element.20), channel_id=1, source_target_pairs={{0,16},{1,17},{2,18},{3,19},{4,20},{5,21},{6,22},{7,23},{8,24},{9,... | collective-permute-start | bytes 147464 | tf_op jit(solution)/shard_map/ppermute | solution.py:31
  37.4 1.5 %collective-permute-start.10 = (f32[32,384]{1,0:T(8,128)S(1)}, f32[32,384]{1,0:T(8,128)S(1)}, u32[]{:S(2)}, u32[]{:S(2)}) collective-permute-start(f32[32,384]{1,0:T(8,128)S(1)} %get-tuple-element.21), channel_id=1, source_target_pairs={{0,24},{1,25},{2,26},{3,27},{4,28},{5,29},{6,30},{7,31},{8,16},{9,... | collective-permute-start | bytes 147464 | tf_op jit(solution)/shard_map/ppermute | solution.py:31
  38.9 0.6 %collective-permute-done.8.refs_1_ = f32[32,384]{1,0:T(8,128)S(1)} collective-permute-done((f32[32,384]{1,0:T(8,128)S(1)}, f32[32,384]{1,0:T(8,128)S(1)}, u32[]{:S(2)}, u32[]{:S(2)}) %collective-permute-start.8) | collective-permute-done | bytes 49184 | tf_op jit(solution)/shard_map/ppermute | solution.py:31
  39.5 1.8 %collective-permute-done.9.refs_2_ = f32[32,384]{1,0:T(8,128)S(1)} collective-permute-done((f32[32,384]{1,0:T(8,128)S(1)}, f32[32,384]{1,0:T(8,128)S(1)}, u32[]{:S(2)}, u32[]{:S(2)}) %collective-permute-start.9) | collective-permute-done | bytes 49184 | tf_op jit(solution)/shard_map/ppermute | solution.py:31
  41.3 1.1 %collective-permute-done.10.refs_3_ = f32[32,384]{1,0:T(8,128)S(1)} collective-permute-done((f32[32,384]{1,0:T(8,128)S(1)}, f32[32,384]{1,0:T(8,128)S(1)}, u32[]{:S(2)}, u32[]{:S(2)}) %collective-permute-start.10) | collective-permute-done | bytes 49184 | tf_op jit(solution)/shard_map/ppermute | solution.py:31
  42.4 0.1 merge.3
  42.5 0.2 collective-permute-start.11
  42.7 2.3 %collective-permute-start.12 = (f32[8,384]{1,0:T(8,128)S(1)}, f32[8,384]{1,0:T(8,128)S(1)}, u32[]{:S(2)}, u32[]{:S(2)}) collective-permute-start(f32[8,384]{1,0:T(8,128)S(1)} %get-tuple-element.24), channel_id=1, source_target_pairs={{0,2},{1,3},{2,0},{3,1},{4,6},{5,7},{6,4},{7,5},{8,10},{9,11},{10,... | collective-permute-start | bytes 36872 | tf_op jit(solution)/shard_map/ppermute | solution.py:31
  45.0 1.9 %collective-permute-start.13 = (f32[8,384]{1,0:T(8,128)S(1)}, f32[8,384]{1,0:T(8,128)S(1)}, u32[]{:S(2)}, u32[]{:S(2)}) collective-permute-start(f32[8,384]{1,0:T(8,128)S(1)} %get-tuple-element.25), channel_id=1, source_target_pairs={{0,3},{1,2},{2,1},{3,0},{4,7},{5,6},{6,5},{7,4},{8,11},{9,10},{10,... | collective-permute-start | bytes 36872 | tf_op jit(solution)/shard_map/ppermute | solution.py:31
  47.0 0.3 collective-permute-done.12.refs_2_
  47.3 3.2 %collective-permute-done.13.refs_3_ = f32[8,384]{1,0:T(8,128)S(1)} collective-permute-done((f32[8,384]{1,0:T(8,128)S(1)}, f32[8,384]{1,0:T(8,128)S(1)}, u32[]{:S(2)}, u32[]{:S(2)}) %collective-permute-start.13) | collective-permute-done | bytes 12320 | tf_op jit(solution)/shard_map/ppermute | solution.py:31
  50.5 0.8 %finish.1 = (f32[8,256]{1,0:T(8,128)}, f32[1,8]{1,0:T(1,128)}, f32[8,32]{1,0:T(8,128)}) custom-call(s32[8,32]{1,0:T(8,128)S(1)} %copy-done, f32[8,384]{1,0:T(8,128)S(1)} %get-tuple-element.22.refs_0_, f32[8,384]{1,0:T(8,128)S(1)} %collective-permute-done.11.refs_1_, f32[8,384]{1,0:T(8,128)S(1)} %collective-permute-done.12.refs_2_, ...), custom_call_target="tpu_custom_call" | custom-call | tf_op jit(solution)/shard_map/finish/pallas_call | solution.py:281
  (8 shorter events, 0.1 us)
Async XLA Ops:
  1.6 7.1 %collective-permute-start.2 = (bf16[8,2176]{1,0:T(8,128)(2,1)S(1)}, bf16[8,2176]{1,0:T(8,128)(2,1)S(1)}, u32[]{:S(2)}, u32[]{:S(2)}) collective-permute-start(bf16[8,2176]{1,0:T(8,128)(2,1)S(1)} %pack.1.refs_0_), channel_id=1, source_target_pairs={{0,3},{1,2},{2,1},{3,0},{4,7},{5,6},{6,5},{7,4},{8,11},{9,10},{10,... | collective-permute-start | bytes 104456 | tf_op jit(solution)/shard_map/ppermute | solution.py:31
  6.8 4.8 %collective-permute-start.1 = (bf16[8,2176]{1,0:T(8,128)(2,1)S(1)}, bf16[8,2176]{1,0:T(8,128)(2,1)S(1)}, u32[]{:S(2)}, u32[]{:S(2)}) collective-permute-start(bf16[8,2176]{1,0:T(8,128)(2,1)S(1)} %pack.1.refs_0_), channel_id=1, source_target_pairs={{0,2},{1,3},{2,0},{3,1},{4,6},{5,7},{6,4},{7,5},{8,10},{9,11},{10,... | collective-permute-start | bytes 104456 | tf_op jit(solution)/shard_map/ppermute | solution.py:31
  6.8 4.8 %collective-permute-start = (bf16[8,2176]{1,0:T(8,128)(2,1)S(1)}, bf16[8,2176]{1,0:T(8,128)(2,1)S(1)}, u32[]{:S(2)}, u32[]{:S(2)}) collective-permute-start(bf16[8,2176]{1,0:T(8,128)(2,1)S(1)} %pack.1.refs_0_), channel_id=1, source_target_pairs={{0,1},{1,0},{2,3},{3,2},{4,5},{5,4},{6,7},{7,6},{8,9},{9,8},{10,11... | collective-permute-start | bytes 104456 | tf_op jit(solution)/shard_map/ppermute | solution.py:31
  11.6 7.5 %collective-permute-start.5 = (bf16[32,2176]{1,0:T(8,128)(2,1)S(1)}, bf16[32,2176]{1,0:T(8,128)(2,1)S(1)}, u32[]{:S(2)}, u32[]{:S(2)}) collective-permute-start(bf16[32,2176]{1,0:T(8,128)(2,1)S(1)} %join.2.refs_0_), channel_id=1, source_target_pairs={{0,24},{1,25},{2,26},{3,27},{4,28},{5,29},{6,30},{7,31},{8,16},{9,... | collective-permute-start | bytes 417800 | tf_op jit(solution)/shard_map/ppermute | solution.py:31
  14.1 5.8 %collective-permute-start.4 = (bf16[32,2176]{1,0:T(8,128)(2,1)S(1)}, bf16[32,2176]{1,0:T(8,128)(2,1)S(1)}, u32[]{:S(2)}, u32[]{:S(2)}) collective-permute-start(bf16[32,2176]{1,0:T(8,128)(2,1)S(1)} %join.2.refs_0_), channel_id=1, source_target_pairs={{0,16},{1,17},{2,18},{3,19},{4,20},{5,21},{6,22},{7,23},{8,24},{9,... | collective-permute-start | bytes 417800 | tf_op jit(solution)/shard_map/ppermute | solution.py:31
  14.6 5.3 %collective-permute-start.3 = (bf16[32,2176]{1,0:T(8,128)(2,1)S(1)}, bf16[32,2176]{1,0:T(8,128)(2,1)S(1)}, u32[]{:S(2)}, u32[]{:S(2)}) collective-permute-start(bf16[32,2176]{1,0:T(8,128)(2,1)S(1)} %join.2.refs_0_), channel_id=1, source_target_pairs={{0,8},{1,9},{2,10},{3,11},{4,12},{5,13},{6,14},{7,15},{8,0},{9,1},... | collective-permute-start | bytes 417800 | tf_op jit(solution)/shard_map/ppermute | solution.py:31
  20.0 7.9 %collective-permute-start.6 = (bf16[128,2176]{1,0:T(8,128)(2,1)S(1)}, bf16[128,2176]{1,0:T(8,128)(2,1)S(1)}, u32[]{:S(2)}, u32[]{:S(2)}) collective-permute-start(bf16[128,2176]{1,0:T(8,128)(2,1)S(1)} %join.3.x_ref), channel_id=1, source_target_pairs={{0,4},{1,5},{2,6},{3,7},{4,0},{5,1},{6,2},{7,3},{8,12},{9,13},{10,... | collective-permute-start | bytes 1671176 | tf_op jit(solution)/shard_map/ppermute | solution.py:31
  27.9 22.7 %copy-start = (s32[8,32]{1,0:T(8,128)S(1)}, s32[8,32]{1,0:T(8,128)}, u32[]{:S(2)}) copy-start(s32[8,32]{1,0:T(8,128)} %owner_ref.1) | copy-start | bytes 3076
  33.6 1.6 %collective-permute-start.7 = (f32[128,384]{1,0:T(8,128)S(1)}, f32[128,384]{1,0:T(8,128)S(1)}, u32[]{:S(2)}, u32[]{:S(2)}) collective-permute-start(f32[128,384]{1,0:T(8,128)S(1)} %get-tuple-element.17), channel_id=1, source_target_pairs={{0,4},{1,5},{2,6},{3,7},{4,0},{5,1},{6,2},{7,3},{8,12},{9,13},{10,... | collective-permute-start | bytes 589832 | tf_op jit(solution)/shard_map/ppermute | solution.py:31
  35.4 4.2 %collective-permute-start.8 = (f32[32,384]{1,0:T(8,128)S(1)}, f32[32,384]{1,0:T(8,128)S(1)}, u32[]{:S(2)}, u32[]{:S(2)}) collective-permute-start(f32[32,384]{1,0:T(8,128)S(1)} %get-tuple-element.19), channel_id=1, source_target_pairs={{0,8},{1,9},{2,10},{3,11},{4,12},{5,13},{6,14},{7,15},{8,0},{9,1},... | collective-permute-start | bytes 147464 | tf_op jit(solution)/shard_map/ppermute | solution.py:31
  36.7 4.6 %collective-permute-start.9 = (f32[32,384]{1,0:T(8,128)S(1)}, f32[32,384]{1,0:T(8,128)S(1)}, u32[]{:S(2)}, u32[]{:S(2)}) collective-permute-start(f32[32,384]{1,0:T(8,128)S(1)} %get-tuple-element.20), channel_id=1, source_target_pairs={{0,16},{1,17},{2,18},{3,19},{4,20},{5,21},{6,22},{7,23},{8,24},{9,... | collective-permute-start | bytes 147464 | tf_op jit(solution)/shard_map/ppermute | solution.py:31
  37.4 5.0 %collective-permute-start.10 = (f32[32,384]{1,0:T(8,128)S(1)}, f32[32,384]{1,0:T(8,128)S(1)}, u32[]{:S(2)}, u32[]{:S(2)}) collective-permute-start(f32[32,384]{1,0:T(8,128)S(1)} %get-tuple-element.21), channel_id=1, source_target_pairs={{0,24},{1,25},{2,26},{3,27},{4,28},{5,29},{6,30},{7,31},{8,16},{9,... | collective-permute-start | bytes 147464 | tf_op jit(solution)/shard_map/ppermute | solution.py:31
  42.5 4.5 %collective-permute-start.11 = (f32[8,384]{1,0:T(8,128)S(1)}, f32[8,384]{1,0:T(8,128)S(1)}, u32[]{:S(2)}, u32[]{:S(2)}) collective-permute-start(f32[8,384]{1,0:T(8,128)S(1)} %get-tuple-element.23), channel_id=1, source_target_pairs={{0,1},{1,0},{2,3},{3,2},{4,5},{5,4},{6,7},{7,6},{8,9},{9,8},{10,11... | collective-permute-start | bytes 36872 | tf_op jit(solution)/shard_map/ppermute | solution.py:31
  42.7 4.6 %collective-permute-start.12 = (f32[8,384]{1,0:T(8,128)S(1)}, f32[8,384]{1,0:T(8,128)S(1)}, u32[]{:S(2)}, u32[]{:S(2)}) collective-permute-start(f32[8,384]{1,0:T(8,128)S(1)} %get-tuple-element.24), channel_id=1, source_target_pairs={{0,2},{1,3},{2,0},{3,1},{4,6},{5,7},{6,4},{7,5},{8,10},{9,11},{10,... | collective-permute-start | bytes 36872 | tf_op jit(solution)/shard_map/ppermute | solution.py:31
  45.0 5.5 %collective-permute-start.13 = (f32[8,384]{1,0:T(8,128)S(1)}, f32[8,384]{1,0:T(8,128)S(1)}, u32[]{:S(2)}, u32[]{:S(2)}) collective-permute-start(f32[8,384]{1,0:T(8,128)S(1)} %get-tuple-element.25), channel_id=1, source_target_pairs={{0,3},{1,2},{2,1},{3,0},{4,7},{5,6},{6,5},{7,4},{8,11},{9,10},{10,... | collective-permute-start | bytes 36872 | tf_op jit(solution)/shard_map/ppermute | solution.py:31

commit v3 on v2

--- a/solution.py
+++ b/solution.py
@@ -10,6 +10,7 @@
 PREFIX = 256
 AXES = ("index", "query")
 RADIX = 64
+LOG2E = 1.4426950408889634
 
 
 def xor_stages(index_size, query_size):
@@ -96,12 +97,12 @@
     copies[0].wait()
     copies[1].wait()
     lane = lax.broadcasted_iota(jnp.int32, (owner_ref.shape[0], lanes), 1)
+    slot = jnp.where(lane < owners, lane, lane - owners)
     table = jnp.zeros(lane.shape, jnp.int32)
-    for k in range(owner_ref.shape[1]):
-        own = owner_ref[:, k : k + 1]
-        row = row_ref[:, k : k + 1] + 1
-        table += jnp.where(lane == own, row // RADIX, 0)
-        table += jnp.where(lane == own + owners, row % RADIX, 0)
+    own, row = owner_ref[...], row_ref[...] + 1
+    for k in range(own.shape[1]):
+        table = jnp.where(slot == own[:, k : k + 1], row[:, k : k + 1], table)
+    table = jnp.where(lane < owners, table // RADIX, table % RADIX)
     out_ref[:, width:] = table.astype(jnp.float32).astype(jnp.bfloat16)
     copies[2].wait()
 
@@ -137,6 +138,14 @@
         logit_ref[:, at] = logits
         for s in range(chunk // 128):
             best = jnp.maximum(best, logits[:, s * 128 : (s + 1) * 128])
+
+    def rest_of(c):
+        ref, own = rows[c]
+        return lax.dot_general(
+            g_ref[:, PREFIX:width], ref[own, PREFIX:], contract, preferred_element_type=jnp.float32
+        )
+
+    ahead = rest_of(0)
     top = jnp.max(best, axis=1, keepdims=True)
     acc = jnp.zeros((n_q, PREFIX), jnp.float32)
     total = jnp.zeros((n_q, 128), jnp.float32)
@@ -144,14 +153,13 @@
     for c in range(n_chunks):
         at = slice(c * chunk, (c + 1) * chunk)
         ref, own = rows[c]
-        full = lax.dot_general(
-            g_ref[:, PREFIX:width], ref[own, PREFIX:], contract, preferred_element_type=jnp.float32
-        )
-        full = full + logit_ref[:, at]
+        full, ahead = ahead, rest_of(c + 1) if c + 1 < n_chunks else None
+        logits = logit_ref[:, at]
+        full = full + logits
         for s in range(chunk // 128):
             part = full[:, s * 128 : (s + 1) * 128]
             score += jnp.where(col + (c * chunk + s * 128) == want, part, 0.0)
-        weights = jnp.exp((logit_ref[:, at] - top) * scale)
+        weights = jnp.exp2((logits - top) * (scale * LOG2E))
         for s in range(chunk // 128):
             total += weights[:, s * 128 : (s + 1) * 128]
         acc += jnp.dot(
@@ -231,7 +239,7 @@
     )(*in_hbm(queries, cand_owner, cand_row))
     r_dev = slab.shape[0]
     chunk = r_dev // 16
-    cuts = [0, 4 * chunk, 14 * chunk, r_dev]
+    cuts = [0, 3 * chunk, 14 * chunk, r_dev]
     pieces = []
     for offs in stages[:-1]:
         got = swaps([x] * len(offs), offs, devices)

time: 51.6 us -> 51.4 us (level)
  no operation moved by 1% of the time
where the time goes in v3:
time: 51.4 us; the launch traced here: 51.1 us
  starting transfers between devices  18 us (35%)
  waiting for transfers between devices  17 us (33%)
  Pallas kernels  15.4 us (30%)
  between operations  0.73 us (1%)
    ppermute x14, starting transfers between devices, swap(): return lax.ppermute(x, AXES, [(d, d ^ off) for d in range(devices)])  18 us
    ppermute x14, waiting for transfers between devices, swap(): return lax.ppermute(x, AXES, [(d, d ^ off) for d in range(devices)])  17 us
    pallas_call x3, Pallas kernels, load(): pl.pallas_call(functools.partial(load_body, first=first), in_specs=[pl.Bl...  7.79 us
    pallas_call x1, Pallas kernels, on_device(): pl.pallas_call(functools.partial(score_body, width=width, owners=owners,...  5.62 us
  transfers between devices with their start and end apart: 14, of which 10 were waited for; matrix products, arithmetic and copies ran while one was open for 0% of the time, Pallas kernels for 15%

profile of v3, /device:TPU:0, one launch (start us, length us, event | category | flops | bytes accessed | tf_op | source)
XLA Modules:
  0.0 51.1 jit_solution(5135110471174583257)
XLA Ops:
  0.6 0.9 %pack.1.refs_0_ = bf16[8,2176]{1,0:T(8,128)(2,1)S(1)} custom-call(bf16[8,2048]{1,0:T(8,128)(2,1)} %q_hbm.1, s32[8,32]{1,0:T(8,128)} %owner_ref.1, s32[8,32]{1,0:T(8,128)} %row_hbm.1), custom_call_target="tpu_custom_call" | custom-call | tf_op jit(solution)/shard_map/pack/pallas_call | solution.py:228
  1.6 5.1 %collective-permute-start.2 = (bf16[8,2176]{1,0:T(8,128)(2,1)S(1)}, bf16[8,2176]{1,0:T(8,128)(2,1)S(1)}, u32[]{:S(2)}, u32[]{:S(2)}) collective-permute-start(bf16[8,2176]{1,0:T(8,128)(2,1)S(1)} %pack.1.refs_0_), channel_id=1, source_target_pairs={{0,3},{1,2},{2,1},{3,0},{4,7},{5,6},{6,5},{7,4},{8,11},{9,10},{10,... | collective-permute-start | bytes 104456 | tf_op jit(solution)/shard_map/ppermute | solution.py:32
  6.7 0.6 %collective-permute-start = (bf16[8,2176]{1,0:T(8,128)(2,1)S(1)}, bf16[8,2176]{1,0:T(8,128)(2,1)S(1)}, u32[]{:S(2)}, u32[]{:S(2)}) collective-permute-start(bf16[8,2176]{1,0:T(8,128)(2,1)S(1)} %pack.1.refs_0_), channel_id=1, source_target_pairs={{0,1},{1,0},{2,3},{3,2},{4,5},{5,4},{6,7},{7,6},{8,9},{9,8},{10,11... | collective-permute-start | bytes 104456 | tf_op jit(solution)/shard_map/ppermute | solution.py:32
  7.3 1.3 %collective-permute-done.2.refs_3_ = bf16[8,2176]{1,0:T(8,128)(2,1)S(1)} collective-permute-done((bf16[8,2176]{1,0:T(8,128)(2,1)S(1)}, bf16[8,2176]{1,0:T(8,128)(2,1)S(1)}, u32[]{:S(2)}, u32[]{:S(2)}) %collective-permute-start.2) | collective-permute-done | bytes 34848 | tf_op jit(solution)/shard_map/ppermute | solution.py:32
  8.6 2.9 %collective-permute-done.1.refs_2_ = bf16[8,2176]{1,0:T(8,128)(2,1)S(1)} collective-permute-done((bf16[8,2176]{1,0:T(8,128)(2,1)S(1)}, bf16[8,2176]{1,0:T(8,128)(2,1)S(1)}, u32[]{:S(2)}, u32[]{:S(2)}) %collective-permute-start.1) | collective-permute-done | bytes 34848 | tf_op jit(solution)/shard_map/ppermute | solution.py:32
  11.5 2.5 %collective-permute-start.5 = (bf16[32,2176]{1,0:T(8,128)(2,1)S(1)}, bf16[32,2176]{1,0:T(8,128)(2,1)S(1)}, u32[]{:S(2)}, u32[]{:S(2)}) collective-permute-start(bf16[32,2176]{1,0:T(8,128)(2,1)S(1)} %join.2.refs_0_), channel_id=1, source_target_pairs={{0,24},{1,25},{2,26},{3,27},{4,28},{5,29},{6,30},{7,31},{8,16},{9,... | collective-permute-start | bytes 417800 | tf_op jit(solution)/shard_map/ppermute | solution.py:32
  14.1 0.5 collective-permute-start.4
  14.6 0.5 %collective-permute-start.3 = (bf16[32,2176]{1,0:T(8,128)(2,1)S(1)}, bf16[32,2176]{1,0:T(8,128)(2,1)S(1)}, u32[]{:S(2)}, u32[]{:S(2)}) collective-permute-start(bf16[32,2176]{1,0:T(8,128)(2,1)S(1)} %join.2.refs_0_), channel_id=1, source_target_pairs={{0,8},{1,9},{2,10},{3,11},{4,12},{5,13},{6,14},{7,15},{8,0},{9,1},... | collective-permute-start | bytes 417800 | tf_op jit(solution)/shard_map/ppermute | solution.py:32
  15.1 3.9 %collective-permute-done.5.refs_3_ = bf16[32,2176]{1,0:T(8,128)(2,1)S(1)} collective-permute-done((bf16[32,2176]{1,0:T(8,128)(2,1)S(1)}, bf16[32,2176]{1,0:T(8,128)(2,1)S(1)}, u32[]{:S(2)}, u32[]{:S(2)}) %collective-permute-start.5) | collective-permute-done | bytes 139296 | tf_op jit(solution)/shard_map/ppermute | solution.py:32
  19.1 0.8 %collective-permute-done.4.refs_2_ = bf16[32,2176]{1,0:T(8,128)(2,1)S(1)} collective-permute-done((bf16[32,2176]{1,0:T(8,128)(2,1)S(1)}, bf16[32,2176]{1,0:T(8,128)(2,1)S(1)}, u32[]{:S(2)}, u32[]{:S(2)}) %collective-permute-start.4) | collective-permute-done | bytes 139296 | tf_op jit(solution)/shard_map/ppermute | solution.py:32
  19.9 0.1 collective-permute-start.6
  20.0 1.6 %load.5.rows_c = bf16[512,2048]{1,0:T(8,128)(2,1)S(1)} custom-call(bf16[4096,2048]{1,0:T(8,128)(2,1)} %from_ref.5), custom_call_target="tpu_custom_call" | custom-call | bytes 2097152 | tf_op jit(solution)/shard_map/load/pallas_call | solution.py:76
  21.6 1.9 %load.3.rows_a = bf16[768,2048]{1,0:T(8,128)(2,1)S(1)} custom-call(bf16[4096,2048]{1,0:T(8,128)(2,1)} %from_ref.5), custom_call_target="tpu_custom_call" | custom-call | bytes 3145728 | tf_op jit(solution)/shard_map/load/pallas_call | solution.py:76
  23.5 4.3 %load.4.rows_b = bf16[2816,2048]{1,0:T(8,128)(2,1)S(1)} custom-call(bf16[4096,2048]{1,0:T(8,128)(2,1)} %from_ref.5), custom_call_target="tpu_custom_call" | custom-call | bytes 11534336 | tf_op jit(solution)/shard_map/load/pallas_call | solution.py:76
  27.8 0.0 copy-start
  27.8 5.6 %score.1 = (f32[128,384]{1,0:T(8,128)S(1)}, f32[128,384]{1,0:T(8,128)S(1)}) custom-call(bf16[128,2176]{1,0:T(8,128)(2,1)S(1)} %join.3.x_ref, bf16[128,2176]{1,0:T(8,128)(2,1)S(1)} %collective-permute-done.6.y_ref, bf16[768,2048]{1,0:T(8,128)(2,1)S(1)} %load.3.rows_a, bf16[2816,2048]{1,0:T(8,128)(2,1)S(1)} %load.4.rows_b, bf16[512,2048]{1,0:T(8,128)(2,1)S(1)} %load.5.rows_c), custom_call_target="tpu_custom_call" | custom-call | tf_op jit(solution)/shard_map/score/pallas_call | solution.py:265
  33.4 0.6 %collective-permute-start.7 = (f32[128,384]{1,0:T(8,128)S(1)}, f32[128,384]{1,0:T(8,128)S(1)}, u32[]{:S(2)}, u32[]{:S(2)}) collective-permute-start(f32[128,384]{1,0:T(8,128)S(1)} %get-tuple-element.17), channel_id=1, source_target_pairs={{0,4},{1,5},{2,6},{3,7},{4,0},{5,1},{6,2},{7,3},{8,12},{9,13},{10,... | collective-permute-start | bytes 589832 | tf_op jit(solution)/shard_map/ppermute | solution.py:32
  34.0 1.1 %collective-permute-done.7.refs_1_ = f32[128,384]{1,0:T(8,128)S(1)} collective-permute-done((f32[128,384]{1,0:T(8,128)S(1)}, f32[128,384]{1,0:T(8,128)S(1)}, u32[]{:S(2)}, u32[]{:S(2)}) %collective-permute-start.7) | collective-permute-done | bytes 196640 | tf_op jit(solution)/shard_map/ppermute | solution.py:32
  35.1 0.1 merge.2
  35.2 1.3 %collective-permute-start.8 = (f32[32,384]{1,0:T(8,128)S(1)}, f32[32,384]{1,0:T(8,128)S(1)}, u32[]{:S(2)}, u32[]{:S(2)}) collective-permute-start(f32[32,384]{1,0:T(8,128)S(1)} %get-tuple-element.19), channel_id=1, source_target_pairs={{0,8},{1,9},{2,10},{3,11},{4,12},{5,13},{6,14},{7,15},{8,0},{9,1},... | collective-permute-start | bytes 147464 | tf_op jit(solution)/shard_map/ppermute | solution.py:32
  36.5 0.7 %collective-permute-start.9 = (f32[32,384]{1,0:T(8,128)S(1)}, f32[32,384]{1,0:T(8,128)S(1)}, u32[]{:S(2)}, u32[]{:S(2)}) collective-permute-start(f32[32,384]{1,0:T(8,128)S(1)} %get-tuple-element.20), channel_id=1, source_target_pairs={{0,16},{1,17},{2,18},{3,19},{4,20},{5,21},{6,22},{7,23},{8,24},{9,... | collective-permute-start | bytes 147464 | tf_op jit(solution)/shard_map/ppermute | solution.py:32
  37.2 1.5 %collective-permute-start.10 = (f32[32,384]{1,0:T(8,128)S(1)}, f32[32,384]{1,0:T(8,128)S(1)}, u32[]{:S(2)}, u32[]{:S(2)}) collective-permute-start(f32[32,384]{1,0:T(8,128)S(1)} %get-tuple-element.21), channel_id=1, source_target_pairs={{0,24},{1,25},{2,26},{3,27},{4,28},{5,29},{6,30},{7,31},{8,16},{9,... | collective-permute-start | bytes 147464 | tf_op jit(solution)/shard_map/ppermute | solution.py:32
  38.7 0.6 %collective-permute-done.8.refs_1_ = f32[32,384]{1,0:T(8,128)S(1)} collective-permute-done((f32[32,384]{1,0:T(8,128)S(1)}, f32[32,384]{1,0:T(8,128)S(1)}, u32[]{:S(2)}, u32[]{:S(2)}) %collective-permute-start.8) | collective-permute-done | bytes 49184 | tf_op jit(solution)/shard_map/ppermute | solution.py:32
  39.3 1.8 %collective-permute-done.9.refs_2_ = f32[32,384]{1,0:T(8,128)S(1)} collective-permute-done((f32[32,384]{1,0:T(8,128)S(1)}, f32[32,384]{1,0:T(8,128)S(1)}, u32[]{:S(2)}, u32[]{:S(2)}) %collective-permute-start.9) | collective-permute-done | bytes 49184 | tf_op jit(solution)/shard_map/ppermute | solution.py:32
  41.1 1.0 %collective-permute-done.10.refs_3_ = f32[32,384]{1,0:T(8,128)S(1)} collective-permute-done((f32[32,384]{1,0:T(8,128)S(1)}, f32[32,384]{1,0:T(8,128)S(1)}, u32[]{:S(2)}, u32[]{:S(2)}) %collective-permute-start.10) | collective-permute-done | bytes 49184 | tf_op jit(solution)/shard_map/ppermute | solution.py:32
  42.2 0.1 merge.3
  42.3 0.2 collective-permute-start.11
  42.5 2.3 %collective-permute-start.12 = (f32[8,384]{1,0:T(8,128)S(1)}, f32[8,384]{1,0:T(8,128)S(1)}, u32[]{:S(2)}, u32[]{:S(2)}) collective-permute-start(f32[8,384]{1,0:T(8,128)S(1)} %get-tuple-element.24), channel_id=1, source_target_pairs={{0,2},{1,3},{2,0},{3,1},{4,6},{5,7},{6,4},{7,5},{8,10},{9,11},{10,... | collective-permute-start | bytes 36872 | tf_op jit(solution)/shard_map/ppermute | solution.py:32
  44.8 1.9 %collective-permute-start.13 = (f32[8,384]{1,0:T(8,128)S(1)}, f32[8,384]{1,0:T(8,128)S(1)}, u32[]{:S(2)}, u32[]{:S(2)}) collective-permute-start(f32[8,384]{1,0:T(8,128)S(1)} %get-tuple-element.25), channel_id=1, source_target_pairs={{0,3},{1,2},{2,1},{3,0},{4,7},{5,6},{6,5},{7,4},{8,11},{9,10},{10,... | collective-permute-start | bytes 36872 | tf_op jit(solution)/shard_map/ppermute | solution.py:32
  46.8 0.3 collective-permute-done.12.refs_2_
  47.1 3.2 %collective-permute-done.13.refs_3_ = f32[8,384]{1,0:T(8,128)S(1)} collective-permute-done((f32[8,384]{1,0:T(8,128)S(1)}, f32[8,384]{1,0:T(8,128)S(1)}, u32[]{:S(2)}, u32[]{:S(2)}) %collective-permute-start.13) | collective-permute-done | bytes 12320 | tf_op jit(solution)/shard_map/ppermute | solution.py:32
  50.3 0.8 %finish.1 = (f32[8,256]{1,0:T(8,128)}, f32[1,8]{1,0:T(1,128)}, f32[8,32]{1,0:T(8,128)}) custom-call(s32[8,32]{1,0:T(8,128)S(1)} %copy-done, f32[8,384]{1,0:T(8,128)S(1)} %get-tuple-element.22.refs_0_, f32[8,384]{1,0:T(8,128)S(1)} %collective-permute-done.11.refs_1_, f32[8,384]{1,0:T(8,128)S(1)} %collective-permute-done.12.refs_2_, ...), custom_call_target="tpu_custom_call" | custom-call | tf_op jit(solution)/shard_map/finish/pallas_call | solution.py:289
  (8 shorter events, 0.1 us)
Async XLA Ops:
  1.6 7.1 %collective-permute-start.2 = (bf16[8,2176]{1,0:T(8,128)(2,1)S(1)}, bf16[8,2176]{1,0:T(8,128)(2,1)S(1)}, u32[]{:S(2)}, u32[]{:S(2)}) collective-permute-start(bf16[8,2176]{1,0:T(8,128)(2,1)S(1)} %pack.1.refs_0_), channel_id=1, source_target_pairs={{0,3},{1,2},{2,1},{3,0},{4,7},{5,6},{6,5},{7,4},{8,11},{9,10},{10,... | collective-permute-start | bytes 104456 | tf_op jit(solution)/shard_map/ppermute | solution.py:32
  6.7 4.8 %collective-permute-start.1 = (bf16[8,2176]{1,0:T(8,128)(2,1)S(1)}, bf16[8,2176]{1,0:T(8,128)(2,1)S(1)}, u32[]{:S(2)}, u32[]{:S(2)}) collective-permute-start(bf16[8,2176]{1,0:T(8,128)(2,1)S(1)} %pack.1.refs_0_), channel_id=1, source_target_pairs={{0,2},{1,3},{2,0},{3,1},{4,6},{5,7},{6,4},{7,5},{8,10},{9,11},{10,... | collective-permute-start | bytes 104456 | tf_op jit(solution)/shard_map/ppermute | solution.py:32
  6.7 4.8 %collective-permute-start = (bf16[8,2176]{1,0:T(8,128)(2,1)S(1)}, bf16[8,2176]{1,0:T(8,128)(2,1)S(1)}, u32[]{:S(2)}, u32[]{:S(2)}) collective-permute-start(bf16[8,2176]{1,0:T(8,128)(2,1)S(1)} %pack.1.refs_0_), channel_id=1, source_target_pairs={{0,1},{1,0},{2,3},{3,2},{4,5},{5,4},{6,7},{7,6},{8,9},{9,8},{10,11... | collective-permute-start | bytes 104456 | tf_op jit(solution)/shard_map/ppermute | solution.py:32
  11.5 7.5 %collective-permute-start.5 = (bf16[32,2176]{1,0:T(8,128)(2,1)S(1)}, bf16[32,2176]{1,0:T(8,128)(2,1)S(1)}, u32[]{:S(2)}, u32[]{:S(2)}) collective-permute-start(bf16[32,2176]{1,0:T(8,128)(2,1)S(1)} %join.2.refs_0_), channel_id=1, source_target_pairs={{0,24},{1,25},{2,26},{3,27},{4,28},{5,29},{6,30},{7,31},{8,16},{9,... | collective-permute-start | bytes 417800 | tf_op jit(solution)/shard_map/ppermute | solution.py:32
  14.1 5.8 %collective-permute-start.4 = (bf16[32,2176]{1,0:T(8,128)(2,1)S(1)}, bf16[32,2176]{1,0:T(8,128)(2,1)S(1)}, u32[]{:S(2)}, u32[]{:S(2)}) collective-permute-start(bf16[32,2176]{1,0:T(8,128)(2,1)S(1)} %join.2.refs_0_), channel_id=1, source_target_pairs={{0,16},{1,17},{2,18},{3,19},{4,20},{5,21},{6,22},{7,23},{8,24},{9,... | collective-permute-start | bytes 417800 | tf_op jit(solution)/shard_map/ppermute | solution.py:32
  14.6 5.3 %collective-permute-start.3 = (bf16[32,2176]{1,0:T(8,128)(2,1)S(1)}, bf16[32,2176]{1,0:T(8,128)(2,1)S(1)}, u32[]{:S(2)}, u32[]{:S(2)}) collective-permute-start(bf16[32,2176]{1,0:T(8,128)(2,1)S(1)} %join.2.refs_0_), channel_id=1, source_target_pairs={{0,8},{1,9},{2,10},{3,11},{4,12},{5,13},{6,14},{7,15},{8,0},{9,1},... | collective-permute-start | bytes 417800 | tf_op jit(solution)/shard_map/ppermute | solution.py:32
  19.9 7.9 %collective-permute-start.6 = (bf16[128,2176]{1,0:T(8,128)(2,1)S(1)}, bf16[128,2176]{1,0:T(8,128)(2,1)S(1)}, u32[]{:S(2)}, u32[]{:S(2)}) collective-permute-start(bf16[128,2176]{1,0:T(8,128)(2,1)S(1)} %join.3.x_ref), channel_id=1, source_target_pairs={{0,4},{1,5},{2,6},{3,7},{4,0},{5,1},{6,2},{7,3},{8,12},{9,13},{10,... | collective-permute-start | bytes 1671176 | tf_op jit(solution)/shard_map/ppermute | solution.py:32
  27.8 22.5 %copy-start = (s32[8,32]{1,0:T(8,128)S(1)}, s32[8,32]{1,0:T(8,128)}, u32[]{:S(2)}) copy-start(s32[8,32]{1,0:T(8,128)} %owner_ref.1) | copy-start | bytes 3076
  33.4 1.6 %collective-permute-start.7 = (f32[128,384]{1,0:T(8,128)S(1)}, f32[128,384]{1,0:T(8,128)S(1)}, u32[]{:S(2)}, u32[]{:S(2)}) collective-permute-start(f32[128,384]{1,0:T(8,128)S(1)} %get-tuple-element.17), channel_id=1, source_target_pairs={{0,4},{1,5},{2,6},{3,7},{4,0},{5,1},{6,2},{7,3},{8,12},{9,13},{10,... | collective-permute-start | bytes 589832 | tf_op jit(solution)/shard_map/ppermute | solution.py:32
  35.2 4.2 %collective-permute-start.8 = (f32[32,384]{1,0:T(8,128)S(1)}, f32[32,384]{1,0:T(8,128)S(1)}, u32[]{:S(2)}, u32[]{:S(2)}) collective-permute-start(f32[32,384]{1,0:T(8,128)S(1)} %get-tuple-element.19), channel_id=1, source_target_pairs={{0,8},{1,9},{2,10},{3,11},{4,12},{5,13},{6,14},{7,15},{8,0},{9,1},... | collective-permute-start | bytes 147464 | tf_op jit(solution)/shard_map/ppermute | solution.py:32
  36.5 4.6 %collective-permute-start.9 = (f32[32,384]{1,0:T(8,128)S(1)}, f32[32,384]{1,0:T(8,128)S(1)}, u32[]{:S(2)}, u32[]{:S(2)}) collective-permute-start(f32[32,384]{1,0:T(8,128)S(1)} %get-tuple-element.20), channel_id=1, source_target_pairs={{0,16},{1,17},{2,18},{3,19},{4,20},{5,21},{6,22},{7,23},{8,24},{9,... | collective-permute-start | bytes 147464 | tf_op jit(solution)/shard_map/ppermute | solution.py:32
  37.2 5.0 %collective-permute-start.10 = (f32[32,384]{1,0:T(8,128)S(1)}, f32[32,384]{1,0:T(8,128)S(1)}, u32[]{:S(2)}, u32[]{:S(2)}) collective-permute-start(f32[32,384]{1,0:T(8,128)S(1)} %get-tuple-element.21), channel_id=1, source_target_pairs={{0,24},{1,25},{2,26},{3,27},{4,28},{5,29},{6,30},{7,31},{8,16},{9,... | collective-permute-start | bytes 147464 | tf_op jit(solution)/shard_map/ppermute | solution.py:32
  42.3 4.5 %collective-permute-start.11 = (f32[8,384]{1,0:T(8,128)S(1)}, f32[8,384]{1,0:T(8,128)S(1)}, u32[]{:S(2)}, u32[]{:S(2)}) collective-permute-start(f32[8,384]{1,0:T(8,128)S(1)} %get-tuple-element.23), channel_id=1, source_target_pairs={{0,1},{1,0},{2,3},{3,2},{4,5},{5,4},{6,7},{7,6},{8,9},{9,8},{10,11... | collective-permute-start | bytes 36872 | tf_op jit(solution)/shard_map/ppermute | solution.py:32
  42.5 4.6 %collective-permute-start.12 = (f32[8,384]{1,0:T(8,128)S(1)}, f32[8,384]{1,0:T(8,128)S(1)}, u32[]{:S(2)}, u32[]{:S(2)}) collective-permute-start(f32[8,384]{1,0:T(8,128)S(1)} %get-tuple-element.24), channel_id=1, source_target_pairs={{0,2},{1,3},{2,0},{3,1},{4,6},{5,7},{6,4},{7,5},{8,10},{9,11},{10,... | collective-permute-start | bytes 36872 | tf_op jit(solution)/shard_map/ppermute | solution.py:32
  44.8 5.5 %collective-permute-start.13 = (f32[8,384]{1,0:T(8,128)S(1)}, f32[8,384]{1,0:T(8,128)S(1)}, u32[]{:S(2)}, u32[]{:S(2)}) collective-permute-start(f32[8,384]{1,0:T(8,128)S(1)} %get-tuple-element.25), channel_id=1, source_target_pairs={{0,3},{1,2},{2,1},{3,0},{4,7},{5,6},{6,5},{7,4},{8,11},{9,10},{10,... | collective-permute-start | bytes 36872 | tf_op jit(solution)/shard_map/ppermute | solution.py:32
